TPU v7x, 32 devices: a whole 2x2x4 slice. The times are simulated.
32 devices in a mesh: dp: 8 (over y, x, core), tp: 4 (over z).
Axes of the slice: x: 2, y: 2, z: 4, core: 2. Of those that a mesh axis runs over, the one named last changes fastest.
Arguments:
- block_in: bfloat16 [128, 4, 37632], P('dp', 'tp'), may hold values from -6 to 6
- ln1_gain: float32 [768], P('tp'), may hold values from 0.1 to 1.9
- ln1_shift: float32 [768], P('tp'), may hold values from -1.75 to 1.75
- tok_w1: float32 [196, 384], replicated, may hold values from -0.4375 to 0.4375
- tok_b1: float32 [384], replicated, may hold values from -1.75 to 1.75
- tok_w2: float32 [384, 196], replicated, may hold values from -0.3125 to 0.3125
- tok_b2: float32 [196], replicated, may hold values from -1.75 to 1.75
- ln2_gain: float32 [768], P('tp'), may hold values from 0.1 to 1.9
- ln2_shift: float32 [768], P('tp'), may hold values from -1.75 to 1.75
- ch_w1: float32 [768, 3072], P('dp', 'tp'), may hold values from -0.21875 to 0.21875
- ch_b1: float32 [3072], replicated, may hold values from -1.75 to 1.75
- ch_w2: float32 [3072, 768], P('tp', 'dp'), may hold values from -0.109375 to 0.109375
- ch_b2: float32 [768], replicated, may hold values from -1.75 to 1.75
- group_ids: int32 [128], P('dp'), may hold values from 0 to 63
- out_grad: bfloat16 [128, 4, 37632], P('dp', 'tp'), may hold values from -6 to 6
Outputs:
- block_out: bfloat16 [128, 4, 37632], P('dp', 'tp')
- dx: bfloat16 [128, 4, 37632], P('dp', 'tp')
- group_norms: float32 [64], replicated
- d_ln1_gain: float32 [768], P('tp')
- d_ln1_shift: float32 [768], P('tp')
- d_tok_w1: float32 [196, 384], replicated
- d_tok_b1: float32 [384], replicated
- d_tok_w2: float32 [384, 196], replicated
- d_tok_b2: float32 [196], replicated
- d_ln2_gain: float32 [768], P('tp')
- d_ln2_shift: float32 [768], P('tp')
- d_ch_w1: float32 [768, 3072], P('dp', 'tp')
- d_ch_b1: float32 [3072], replicated
- d_ch_w2: float32 [3072, 768], P('tp', 'dp')
- d_ch_b2: float32 [768], replicated
All inputs are finite; a program needn't handle non-finite values.
Results may differ from a plain program's by a relative error of at most 0.01.
Values may be sent and summed in bfloat16 or wider, within the bound.
A program may use at most 128 MiB of HBM per device.

v0:
```python
import functools
import math

import jax
import jax.numpy as jnp
from jax import lax
from jax.experimental import pallas as pl
from jax.experimental.pallas import tpu as pltpu
from jax.sharding import PartitionSpec as P

MESH = pl.DeviceIdType.MESH


def place():
    dp = lax.axis_index("dp"); t = lax.axis_index("tp")
    c = dp % 2; x = (dp // 2) % 2; y = dp // 4
    def at(yy, xx, cc): return (yy * 2 + xx) * 2 + cc
    return dp, t, dict(S=at(y, x, 1 - c), X=at(y, 1 - x, c), Y=at(1 - y, x, c), D=at(1 - y, 1 - x, c)), (y, x, c)

def others(t):
    first = jnp.where(t == 0, 1, jnp.where(t == 1, 0, jnp.where(t == 2, 3, 2)))
    second = jnp.where(t == 0, 2, jnp.where(t == 1, 2, 1))
    third = jnp.where(t < 2, 3, 0)
    return [first, second, third]

def meet(devices):
    barrier = pltpu.get_barrier_semaphore()
    for device in devices:
        pl.semaphore_signal(barrier, inc=1, device_id=device, device_id_type=MESH)
    pl.semaphore_wait(barrier, len(devices))

def gather_kernel(shard, out, send_sem, recv_sem, local_sem):
    dp, t, near, (y, x, c) = place()
    line = others(t)
    order = [t] + line
    meet([(near["S"], t), (near["X"], t), (near["Y"], t)] + [(dp, p) for p in line])
    started = []
    def send(src, owner, tt, device):
        k = len(started)
        copy = pltpu.make_async_remote_copy(src_ref=src, dst_ref=out.at[:, tt, owner], send_sem=send_sem.at[k],
            recv_sem=recv_sem.at[owner, tt], device_id=device, device_id_type=MESH)
        copy.start(); started.append(copy)
    def arrived(owner, tt):
        ref = out.at[:, tt, owner]
        pltpu.make_async_remote_copy(src_ref=ref, dst_ref=ref, send_sem=send_sem.at[0], recv_sem=recv_sem.at[owner, tt],
            device_id=(dp, t), device_id_type=MESH).wait_recv()
    own = pltpu.make_async_copy(shard, out.at[:, t, dp], local_sem); own.start()
    for p in line: send(shard, dp, t, (dp, p))
    def column(k):
        tt = order[k]
        if k: arrived(dp, tt)
        src = shard if k == 0 else out.at[:, tt, dp]
        send(src, dp, tt, (near["X"], t)); send(src, dp, tt, (near["Y"], t)); send(src, dp, tt, (near["S"], t))
    def neighbours(k):
        tt = order[k]
        first, second = ("X", "Y") if k % 2 == 0 else ("Y", "X")
        arrived(near[first], tt); src = out.at[:, tt, near[first]]
        send(src, near[first], tt, (near[second], t)); send(src, near[first], tt, (near["S"], t))
        arrived(near[second], tt); send(out.at[:, tt, near[second]], near[second], tt, (near["S"], t))
    def diagonal(k):
        tt = order[k]; arrived(near["D"], tt); send(out.at[:, tt, near["D"]], near["D"], tt, (near["S"], t))
    column(0); column(1); neighbours(0); column(2); neighbours(1); diagonal(0); column(3); neighbours(2); diagonal(1)
    neighbours(3); diagonal(2); diagonal(3)
    def at(yy, xx, cc): return (yy * 2 + xx) * 2 + cc
    for k in range(4):
        for yy, xx in ((y, x), (y, 1 - x), (1 - y, x), (1 - y, 1 - x)):
            arrived(at(yy, xx, 1 - c), order[k])
    own.wait()
    for copy in started: copy.wait_send()

def gather_weights(shard, cid=1):
    two, rows, cols = shard.shape
    return pl.pallas_call(gather_kernel,
        out_shape=jax.ShapeDtypeStruct((two, 4, 8, rows, cols), shard.dtype),
        in_specs=[pl.BlockSpec(memory_space=pl.ANY)], out_specs=pl.BlockSpec(memory_space=pl.ANY),
        scratch_shapes=[pltpu.SemaphoreType.DMA((31,)), pltpu.SemaphoreType.DMA((8, 4)), pltpu.SemaphoreType.DMA],
        compiler_params=pltpu.CompilerParams(collective_id=cid, has_side_effects=True))(shard)


F32 = jnp.float32
BF16 = jnp.bfloat16
HALF = 98
GAP = 104
ROWS = 208
LOW = math.sqrt(2.0 / math.pi)
CUBE = 0.044715


def gelu_pair(v):
    square = v * v
    up = 0.5 * jnp.tanh(v * (LOW + (LOW * CUBE) * square)) + 0.5
    value = v * up
    slope = up + value * (1.0 - up) * (2.0 * LOW + (6.0 * LOW * CUBE) * square)
    return value, slope


def turn(v):
    return pltpu.roll(v, 64, 1)


def join_groups(flat, image, store):
    low = lax.broadcasted_iota(jnp.int32, (HALF, 128), 1) < 64
    for p in range(2):
        a = [flat[2 * p, pl.ds(image * HALF, HALF), 128 * j : 128 * j + 128] for j in range(3)]
        b = [flat[2 * p + 1, pl.ds(image * HALF, HALF), 128 * j : 128 * j + 128] for j in range(3)]
        a1, a2, b0, b1 = turn(a[1]), turn(a[2]), turn(b[0]), turn(b[1])
        even = [a[0], jnp.where(low, a[1], b0), jnp.where(low, b0, b1)]
        odd = [jnp.where(low, a1, a2), jnp.where(low, a2, b[1]), b[2]]
        for j in range(3):
            store(0, 384 * p + 128 * j, even[j])
            store(GAP, 384 * p + 128 * j, odd[j])


def split_groups(load, flat, image):
    low = lax.broadcasted_iota(jnp.int32, (HALF, 128), 1) < 64
    for p in range(2):
        e = [load(0, 384 * p + 128 * j) for j in range(3)]
        o = [load(GAP, 384 * p + 128 * j) for j in range(3)]
        e1, e2, o0, o1 = turn(e[1]), turn(e[2]), turn(o[0]), turn(o[1])
        a = [e[0], jnp.where(low, e[1], o0), jnp.where(low, o0, o1)]
        b = [jnp.where(low, e1, e2), jnp.where(low, e2, o[1]), o[2]]
        for j in range(3):
            flat[2 * p, pl.ds(image * HALF, HALF), 128 * j : 128 * j + 128] = a[j]
            flat[2 * p + 1, pl.ds(image * HALF, HALF), 128 * j : 128 * j + 128] = b[j]


def hat(v):
    average = jnp.mean(v, -1, keepdims=True)
    inverse = lax.rsqrt(jnp.mean(v * v, -1, keepdims=True) - average * average + 1e-06)
    return (v - average) * inverse, inverse


def dot(a, b):
    return jnp.dot(a, b, preferred_element_type=F32)


def dot_nt(a, b):
    return lax.dot_general(a, b, (((1,), (1,)), ((), ())), preferred_element_type=F32)


def forward_kernel(shard, xs, ds, lnp, w1t, w2t, b1, b2, cb1, cb2,
                   w_out, g_out, s_out, u_out, hn_out, x_out, dz_out, h_out, t_out, o_out, ln_out,
                   wv, xr, dr, flat, x, xb, u, hn, g, s, h, ts, zs, op, dz, lr,
                   send_sem, recv_sem, x_send, x_recv, d_send, d_recv, l_send, l_recv, own_sem, keep_sem):
    dp, t, near, (y, xx, c) = place()
    line = others(t)
    order = [t] + line

    def at(yy, xxx, cc):
        return (yy * 2 + xxx) * 2 + cc

    started, kept = [], []

    def remote(src, dst, ss, rs, device):
        return pltpu.make_async_remote_copy(src_ref=src, dst_ref=dst, send_sem=ss, recv_sem=rs, device_id=device, device_id_type=MESH)

    def go(copy):
        copy.start()
        started.append(copy)

    def keep(src, dst):
        copy = pltpu.make_async_copy(src, dst, keep_sem.at[len(kept)])
        copy.start()
        kept.append(copy)

    meet([(near["S"], t), (near["X"], t), (near["Y"], t)] + [(dp, p) for p in line])
    sends = [0]

    def send(src, owner, tt, device):
        go(remote(src, wv.at[:, tt, owner], send_sem.at[sends[0]], recv_sem.at[owner, tt], device))
        sends[0] += 1

    def arrived(owner, tt):
        ref = wv.at[:, tt, owner]
        remote(ref, ref, send_sem.at[0], recv_sem.at[owner, tt], (dp, t)).wait_recv()

    own_w = pltpu.make_async_copy(shard, wv.at[:, t, dp], own_sem.at[0])
    own_x = pltpu.make_async_copy(xs.at[t], xr.at[t], own_sem.at[1])
    own_d = pltpu.make_async_copy(ds.at[t], dr.at[t], own_sem.at[2])
    own_l = pltpu.make_async_copy(lnp, lr.at[t], own_sem.at[3])
    for copy in (own_w, own_x, own_d, own_l):
        copy.start()
    for p in line:
        send(shard, dp, t, (dp, p))
    for n, p in enumerate(line):
        go(remote(lnp, lr.at[t], l_send.at[n], l_recv.at[t], (dp, p)))

    def column(k):
        tt = order[k]
        if k:
            arrived(dp, tt)
        src = wv.at[:, tt, dp] if k else shard
        for name in "XYS":
            send(src, dp, tt, (near[name], t))

    def neighbours(k):
        tt = order[k]
        first, second = ("X", "Y") if k % 2 == 0 else ("Y", "X")
        arrived(near[first], tt)
        src = wv.at[:, tt, near[first]]
        send(src, near[first], tt, (near[second], t))
        send(src, near[first], tt, (near["S"], t))
        arrived(near[second], tt)
        send(wv.at[:, tt, near[second]], near[second], tt, (near["S"], t))

    def diagonal(k):
        tt = order[k]
        arrived(near["D"], tt)
        send(wv.at[:, tt, near["D"]], near["D"], tt, (near["S"], t))

    column(0)
    column(1)
    neighbours(0)
    for n, p in enumerate(line):
        go(remote(xs.at[p], xr.at[t], x_send.at[n], x_recv.at[t], (dp, p)))
    column(2)
    neighbours(1)
    diagonal(0)
    column(3)
    neighbours(2)
    diagonal(1)
    neighbours(3)
    diagonal(2)
    diagonal(3)

    own_l.wait()
    for p in line:
        remote(lr.at[p], lr.at[p], l_send.at[0], l_recv.at[p], (dp, t)).wait_recv()
    params = (lr[0] + lr[1]) + (lr[2] + lr[3])
    lr[0] = params
    keep(lr.at[0], ln_out)
    zero = jnp.zeros((GAP - HALF, 768), F32)
    for n in range(4):
        for start in (HALF, GAP + HALF):
            x[n, start : start + GAP - HALF, :] = zero
    own_x.wait()
    for p in line:
        remote(xr.at[p], xr.at[p], x_send.at[0], x_recv.at[p], (dp, t)).wait_recv()
    for n, p in enumerate(line):
        go(remote(ds.at[p], dr.at[t], d_send.at[n], d_recv.at[t], (dp, p)))
    for k in range(4):
        flat[k] = xr[k].astype(F32)
    for n in range(4):
        def put(row, lane, v, n=n):
            x[n, row : row + HALF, lane : lane + 128] = v
        join_groups(flat, n, put)
        xb[n] = x[n].astype(BF16)
    keep(xb, x_out)
    g1, s1, g2, s2 = params[0:1], params[1:2], params[2:3], params[3:4]

    def token(n, carry):
        v = x[n]
        xhat, _ = hat(v)
        a = (xhat * g1 + s1).astype(BF16)
        value, slope = gelu_pair(dot(w1t[...], a) + b1[...])
        low = value.astype(BF16)
        h[n] = low
        ts[n] = slope.astype(BF16)
        r = v + dot(w2t[...], low) + b2[...]
        u[n] = r
        uhat, _ = hat(r)
        hn[n] = (uhat * g2 + s2).astype(BF16)
        return carry

    lax.fori_loop(0, 4, token, 0)
    keep(u, u_out)
    keep(hn, hn_out)
    keep(h, h_out)
    keep(ts, t_out)

    own_w.wait()
    for k in range(4):
        tt = order[k]
        for yy, xxx in ((y, xx), (y, 1 - xx), (1 - y, xx), (1 - y, 1 - xx)):
            arrived(at(yy, xxx, 1 - c), tt)
        keep(wv.at[:, tt], w_out.at[:, tt])

        def block(n, carry, tt=tt, k=k):
            value, slope = gelu_pair(dot(hn[n], wv[0, tt].reshape(768, 768)) + cb1[tt])
            low = value.astype(BF16)
            g[tt, n] = low
            s[tt, n] = slope.astype(BF16)
            part = dot_nt(low, wv[1, tt].reshape(768, 768))
            if k == 0:
                zs[n] = part
            elif k < 3:
                zs[n] += part
            else:
                z = (zs[n] + part + cb2[...]).astype(BF16).astype(F32)
                zs[n] = u[n] + z
            return carry

        lax.fori_loop(0, 4, block, 0)
        keep(g.at[tt], g_out.at[tt])
        keep(s.at[tt], s_out.at[tt])
    for n in range(4):
        split_groups(lambda row, lane, n=n: zs[n, row : row + HALF, lane : lane + 128], flat, n)
    for k in range(4):
        op[k] = flat[k].astype(BF16)
    keep(op, o_out)
    own_d.wait()
    for p in line:
        remote(dr.at[p], dr.at[p], d_send.at[0], d_recv.at[p], (dp, t)).wait_recv()
    for k in range(4):
        flat[k] = dr[k].astype(F32)
    for n in range(4):
        for start in (HALF, GAP + HALF):
            zs[n, start : start + GAP - HALF, :] = zero

        def put_grad(row, lane, v, n=n):
            zs[n, row : row + HALF, lane : lane + 128] = v

        join_groups(flat, n, put_grad)
        dz[n] = zs[n].astype(BF16)
    keep(dz, dz_out)
    for copy in started:
        copy.wait_send()
    for copy in kept:
        copy.wait()


def forward_pass(shard, xs, ds, lnp, w1t, w2t, b1, b2, cb1, cb2):
    any_, vmem = pl.BlockSpec(memory_space=pl.ANY), pl.BlockSpec(memory_space=pltpu.VMEM)
    sds = jax.ShapeDtypeStruct
    dma = pltpu.SemaphoreType.DMA
    wshape = (2, 4, 8, 96, 768)
    act, tok = (4, ROWS, 768), (4, 384, 768)
    packed = (4, 4 * HALF, 384)
    shapes = [(wshape, BF16), ((4,) + act, BF16), ((4,) + act, BF16), (act, F32), (act, BF16), (act, BF16), (act, BF16), (tok, BF16), (tok, BF16), (packed, BF16), ((8, 768), F32)]
    V = pltpu.VMEM
    return pl.pallas_call(forward_kernel,
        out_shape=[sds(*v) for v in shapes],
        in_specs=[any_] * 4 + [vmem] * 6, out_specs=[any_] * len(shapes),
        scratch_shapes=[V(wshape, BF16), V(packed, BF16), V(packed, BF16), V(packed, F32), V(act, F32), V(act, BF16), V(act, F32), V(act, BF16),
            V((4,) + act, BF16), V((4,) + act, BF16), V(tok, BF16), V(tok, BF16), V(act, F32), V(packed, BF16), V(act, BF16), V((4, 8, 768), F32),
            dma((31,)), dma((8, 4)), dma((3,)), dma((4,)), dma((3,)), dma((4,)), dma((3,)), dma((4,)), dma((4,)), dma((24,))],
        compiler_params=pltpu.CompilerParams(collective_id=1, has_side_effects=True, vmem_limit_bytes=60 << 20))(
            shard, xs, ds, lnp, w1t, w2t, b1, b2, cb1, cb2)


PIECE = 48
SMALL = 8 * PIECE


def backward_kernel(bound, w_in, g_in, s_in, u_in, hn_in, x_in, dz_in, h_in, t_in, op, norms, w1, w2, member,
                    o_out, dx_out, w_grad, total_out, fin, group_norms,
                    wv, g, s, u, hn, x, dz, h, ts, hnt, dzt, dq, dhn, gr, flat, dxp,
                    sib, first, second, final, zbuf, small, t_sib, t_chip, t_line,
                    load_sem, slot_sem, own_sem, o_send, o_recv, x_send, x_recv, sib_sem, sib_recv, a_send, a_recv, z_send, z_recv,
                    p_send, p_recv, c_send, c_recv, l_send, l_recv, b_send, b_recv, e_send, e_recv):
    dp, t, near, (y, xx, c) = place()
    line = others(t)
    order = [line[2], line[1], line[0], t]

    def at(yy, xxx, cc):
        return (yy * 2 + xxx) * 2 + cc

    chips = {"O": (y, xx), "X": (y, 1 - xx), "Y": (1 - y, xx), "D": (1 - y, 1 - xx)}
    slot = {"O": 0, "X": 1, "Y": 2, "D": 3}
    started = []

    def remote(src, dst, ss, rs, device):
        return pltpu.make_async_remote_copy(src_ref=src, dst_ref=dst, send_sem=ss, recv_sem=rs, device_id=device, device_id_type=MESH)

    def go(copy):
        copy.start()
        started.append(copy)

    def load(src, dst, n):
        copy = pltpu.make_async_copy(src, dst, load_sem.at[n])
        copy.start()
        return copy

    def fetch(k):
        tt, n = order[k], k % 2
        copies = [pltpu.make_async_copy(w_in.at[:, tt], wv.at[n], slot_sem.at[n, 0]),
                  pltpu.make_async_copy(g_in.at[tt], g.at[n], slot_sem.at[n, 1]),
                  pltpu.make_async_copy(s_in.at[tt], s.at[n], slot_sem.at[n, 2])]
        for copy in copies:
            copy.start()
        return copies

    load_dz = load(dz_in, dz, 0)
    load_hn = load(hn_in, hn, 1)
    slots = {0: fetch(0), 1: fetch(1)}
    later = [load(u_in, u, 2), load(x_in, x, 3), load(h_in, h, 4), load(t_in, ts, 5)]
    meet([(near["S"], t), (near["X"], t), (near["Y"], t), (near["D"], t)] + [(dp, p) for p in line])
    own_o = pltpu.make_async_copy(op.at[t], o_out.at[t], own_sem.at[0])
    own_o.start()
    for n, p in enumerate(line):
        go(remote(op.at[p], o_out.at[t], o_send.at[n], o_recv.at[t], (dp, p)))

    load_dz.wait()
    zero = jnp.zeros((1, 768), F32)
    small[...] = jnp.zeros((SMALL, 768), F32)
    for n in range(4):
        dzt[:, n * ROWS : (n + 1) * ROWS] = dz[n].T
    load_hn.wait()
    for n in range(4):
        hnt[:, n * ROWS : (n + 1) * ROWS] = hn[n].T

    def channel(k):
        n2 = k % 2
        for copy in slots[k]:
            copy.wait()

        def image(n, bias):
            slope = s[n2, n].astype(F32)
            low = (dot(dz[n], wv[n2, 1].reshape(768, 768)) * slope).astype(BF16)
            dq[pl.ds(pl.multiple_of(n * ROWS, 16), ROWS), :] = low
            part = dot_nt(low, wv[n2, 0].reshape(768, 768))
            if k == 0:
                dhn[n] = part
            else:
                dhn[n] += part
            return bias + jnp.sum(low.astype(F32), 0, keepdims=True)

        bias = lax.fori_loop(0, 4, image, zero)
        small[pl.ds(HALF + 1 + order[k], 1), :] = bias
        gr[0, k] = dot(hnt[...], dq[...]).astype(BF16).reshape(8, 96, 768)
        gr[1, k] = dot(dzt[...], g[n2].reshape(4 * ROWS, 768)).astype(BF16).reshape(8, 96, 768)
        if k < 2:
            slots[k + 2] = fetch(k + 2)
        for name in "DXYO":
            n = slot[name]
            go(remote(gr.at[:, k, at(*chips[name], 1 - c)], sib.at[k, n], sib_sem.at[k, n], sib_recv.at[k, n], (near["S"], t)))

    def chip_sum(k, name):
        n = slot[name]
        remote(sib.at[k, n], sib.at[k, n], sib_sem.at[k, n], sib_recv.at[k, n], (near["S"], t)).wait_recv()
        sib[k, n] = (gr[:, k, at(*chips[name], c)].astype(F32) + sib[k, n].astype(F32)).astype(BF16)

    def ways(k):
        return ("X", "Y") if k % 2 == 0 else ("Y", "X")

    def stage_one(k):
        f, s2 = ways(k)
        chip_sum(k, "D")
        go(remote(sib.at[k, 3], first.at[k], a_send.at[k, 0], a_recv.at[k, 0], (near[s2], t)))
        chip_sum(k, s2)
        go(remote(sib.at[k, slot[s2]], second.at[k], a_send.at[k, 1], a_recv.at[k, 1], (near[s2], t)))

    def stage_two(k):
        f, s2 = ways(k)
        chip_sum(k, f)
        remote(first.at[k], first.at[k], a_send.at[k, 0], a_recv.at[k, 0], (near[s2], t)).wait_recv()
        n = slot[f]
        sib[k, n] = (sib[k, n].astype(F32) + first[k].astype(F32)).astype(BF16)
        go(remote(sib.at[k, n], final.at[k], a_send.at[k, 2], a_recv.at[k, 2], (near[f], t)))

    def stage_three(k):
        f, s2 = ways(k)
        chip_sum(k, "O")
        remote(second.at[k], second.at[k], a_send.at[k, 1], a_recv.at[k, 1], (near[s2], t)).wait_recv()
        remote(final.at[k], final.at[k], a_send.at[k, 2], a_recv.at[k, 2], (near[f], t)).wait_recv()
        total = sib[k, 0].astype(F32) + second[k].astype(F32) + final[k].astype(F32)
        if k < 3:
            sib[k, 0] = total.astype(BF16)
            go(remote(sib.at[k, 0], zbuf.at[t], z_send.at[k], z_recv.at[t], (dp, order[k])))
        else:
            w_grad[...] = total

    channel(0)
    channel(1)
    stage_one(0)
    channel(2)
    stage_one(1)
    stage_two(0)
    channel(3)
    stage_one(2)
    stage_two(1)
    stage_three(0)

    for copy in later:
        copy.wait()
    g1, s1, g2 = norms[0:1], norms[1:2], norms[2:3]
    row = lax.broadcasted_iota(jnp.int32, (ROWS, 768), 0)
    ones = jnp.ones((8, 768), BF16)

    def token(n, carry):
        sum_g1, sum_s1, sum_b2 = carry
        d, grad = dhn[n], dz[n].astype(F32)
        uhat, inv_u = hat(u[n])
        pg = jnp.sum(d * uhat, 0, keepdims=True)
        pb = jnp.sum(d, 0, keepdims=True)
        small[208:272, :] += member[n] * pg
        small[272:336, :] += member[n] * pb
        e = d * g2
        du = grad + inv_u * (e - jnp.mean(e, -1, keepdims=True) - uhat * jnp.mean(e * uhat, -1, keepdims=True))
        low = du.astype(BF16)
        dpre = (dot(w2[...], low) * ts[n].astype(F32)).astype(BF16)
        xhat, inv_x = hat(x[n].astype(F32))
        a = jnp.where(row == HALF, 1.0, xhat * g1 + s1).astype(BF16)
        tok1 = dot_nt(a, dpre)
        tok2 = dot_nt(low, h[n])
        for start, size in ((0, HALF + 1), (GAP, HALF)):
            small[start : start + size, 0:384] += tok1[start : start + size]
        for start, size in ((0, HALF), (GAP, HALF)):
            small[start : start + size, 384:768] += tok2[start : start + size]
        da = dot(w1[...], dpre)
        e1 = da * g1
        dhn[n] = du + inv_x * (e1 - jnp.mean(e1, -1, keepdims=True) - xhat * jnp.mean(e1 * xhat, -1, keepdims=True))
        return (sum_g1 + jnp.sum(da * xhat, 0, keepdims=True), sum_s1 + jnp.sum(da, 0, keepdims=True), sum_b2 + dot_nt(ones, low))

    carry = (zero, zero, jnp.zeros((8, ROWS), F32))
    carry = lax.fori_loop(0, 2, token, carry)
    stage_one(3)
    stage_two(2)
    stage_three(1)
    carry = lax.fori_loop(2, 4, token, carry)
    for n in range(4):
        split_groups(lambda r, lane, n=n: dhn[n, r : r + HALF, lane : lane + 128], flat, n)
    for k in range(4):
        dxp[k] = flat[k].astype(BF16)
    own_x = pltpu.make_async_copy(dxp.at[t], dx_out.at[t], own_sem.at[1])
    own_x.start()
    for n, p in enumerate(line):
        go(remote(dxp.at[p], dx_out.at[t], x_send.at[n], x_recv.at[t], (dp, p)))
    small[202:203, :] = carry[0]
    small[203:204, :] = carry[1]
    small[204:205, 0:ROWS] = carry[2][0:1]
    total_dz = zero
    for n in range(4):
        total_dz += jnp.sum(dz[n].astype(F32), 0, keepdims=True)
    small[205:206, :] = total_dz

    chip = dp // 2
    far = [("X", near["X"] // 2), ("Y", near["Y"] // 2), ("D", near["D"] // 2)]

    def part(ref, core, q):
        return ref.at[pl.ds(pl.multiple_of((core * 4 + q) * PIECE, 8), PIECE)]

    def half(ref, core):
        return ref.at[pl.ds(pl.multiple_of(core * 4 * PIECE, 8), 4 * PIECE)]

    go(remote(half(small, 1 - c), t_sib, p_send, p_recv, (near["S"], t)))
    stage_two(3)
    stage_three(2)
    remote(t_sib, t_sib, p_send, p_recv, (near["S"], t)).wait_recv()
    half(small, c)[...] += t_sib[...]
    for n, (name, q) in enumerate(far):
        go(remote(part(small, c, q), t_chip.at[n], c_send.at[n], c_recv.at[n], (near[name], t)))
    stage_three(3)
    total = part(small, c, chip)[...]
    for n in range(3):
        remote(t_chip.at[n], t_chip.at[n], c_send.at[n], c_recv.at[n], (near["S"], t)).wait_recv()
        total = total + t_chip[n]
    t_line[t] = total
    for n, p in enumerate(line):
        go(remote(t_line.at[t], t_line.at[t], l_send.at[n], l_recv.at[t], (dp, p)))
    for p in line:
        remote(t_line.at[p], t_line.at[p], l_send.at[0], l_recv.at[p], (dp, t)).wait_recv()
    own = part(total_out, c, chip)
    own[...] = ((t_line[0] + t_line[1]) + t_line[2]) + t_line[3]
    for n, (name, q) in enumerate(far):
        go(remote(own, own, b_send.at[n], b_recv.at[chip], (near[name], t)))
    go(remote(own, own, e_send.at[3], e_recv.at[chip], (near["S"], t)))
    for p in line:
        remote(zbuf.at[p], zbuf.at[p], z_send.at[0], z_recv.at[p], (dp, t)).wait_recv()
        w_grad[...] += zbuf[p].astype(F32)
    for n, (name, q) in enumerate(far):
        there = part(total_out, c, q)
        remote(there, there, b_send.at[0], b_recv.at[q], (dp, t)).wait_recv()
        go(remote(there, there, e_send.at[n], e_recv.at[q], (near["S"], t)))
    for q in range(4):
        there = part(total_out, 1 - c, q)
        remote(there, there, e_send.at[0], e_recv.at[q], (dp, t)).wait_recv()
    gg, gb = total_out[208:272, :], total_out[272:336, :]
    size = jnp.sqrt(jnp.sum(gg * gg + gb * gb, -1, keepdims=True))
    factor = bound / jnp.maximum(size, bound)
    group_norms[...] = size
    fin[0:1, :] = total_out[202:203, :]
    fin[1:2, :] = total_out[203:204, :]
    fin[2:3, :] = jnp.sum(factor * gg, 0, keepdims=True)
    fin[3:4, :] = jnp.sum(factor * gb, 0, keepdims=True)
    own_o.wait()
    own_x.wait()
    for p in line:
        remote(o_out.at[p], o_out.at[p], o_send.at[0], o_recv.at[p], (dp, t)).wait_recv()
        remote(dx_out.at[p], dx_out.at[p], x_send.at[0], x_recv.at[p], (dp, t)).wait_recv()
    for copy in started:
        copy.wait_send()


def backward_pass(bound, *operands):
    any_, vmem = pl.BlockSpec(memory_space=pl.ANY), pl.BlockSpec(memory_space=pltpu.VMEM)
    sds = jax.ShapeDtypeStruct
    dma = pltpu.SemaphoreType.DMA
    V = pltpu.VMEM
    act, tok, packed, piece = (4, ROWS, 768), (4, 384, 768), (4, 4 * HALF, 384), (2, 96, 768)
    return pl.pallas_call(functools.partial(backward_kernel, bound),
        out_shape=[sds(packed, BF16), sds(packed, BF16), sds(piece, F32), sds((SMALL, 768), F32), sds((8, 768), F32), sds((64, 1), F32)],
        in_specs=[any_] * 10 + [vmem] * 4, out_specs=[any_] * 2 + [vmem] * 4,
        scratch_shapes=[V((2, 2, 8, 96, 768), BF16), V((2,) + act, BF16), V((2,) + act, BF16), V(act, F32), V(act, BF16), V(act, BF16), V(act, BF16),
            V(tok, BF16), V(tok, BF16), V((768, 4 * ROWS), BF16), V((768, 4 * ROWS), BF16), V((4 * ROWS, 768), BF16), V(act, F32),
            V((2, 4, 8, 96, 768), BF16), V(packed, F32), V(packed, BF16),
            V((4, 4) + piece, BF16), V((4,) + piece, BF16), V((4,) + piece, BF16), V((4,) + piece, BF16), V((4,) + piece, BF16),
            V((SMALL, 768), F32), V((4 * PIECE, 768), F32), V((3, PIECE, 768), F32), V((4, PIECE, 768), F32),
            dma((6,)), dma((2, 3)), dma((2,)), dma((3,)), dma((4,)), dma((3,)), dma((4,)), dma((4, 4)), dma((4, 4)), dma((4, 3)), dma((4, 3)), dma((4,)), dma((4,)),
            dma, dma, dma((3,)), dma((3,)), dma((3,)), dma((4,)), dma((3,)), dma((4,)), dma((4,)), dma((4,))],
        compiler_params=pltpu.CompilerParams(collective_id=2, has_side_effects=True, vmem_limit_bytes=62 << 20))(*operands)


def halves(v, axis):
    shape = v.shape
    pairs = v.reshape(shape[:axis] + (HALF, 2) + shape[axis + 1 :])
    pads = [(0, 0)] * v.ndim
    pads[axis] = (0, GAP - HALF)
    parts = [jnp.pad(lax.index_in_dim(pairs, k, axis + 1, keepdims=False), pads) for k in range(2)]
    return jnp.concatenate(parts, axis)


def whole(v, axis):
    parts = [lax.slice_in_dim(v, start, start + HALF, axis=axis) for start in (0, GAP)]
    return jnp.stack(parts, axis + 1).reshape(v.shape[:axis] + (2 * HALF,) + v.shape[axis + 1 :])


S = 196
GROUPS = 64
epsilon = 1e-06
highest = lax.Precision.HIGHEST


def normalised(values):
    average = jnp.mean(values, -1, keepdims=True)
    inverse = lax.rsqrt(jnp.mean(values * values, -1, keepdims=True) - average * average + epsilon)
    return (values - average) * inverse, inverse


def norm_back(grad_hat, normed, inverse):
    return inverse * (
        grad_hat - jnp.mean(grad_hat, -1, keepdims=True) - normed * jnp.mean(grad_hat * normed, -1, keepdims=True)
    )


def general(block_in, ln1_gain, ln1_shift, tok_w1, tok_b1, tok_w2, tok_b2, ln2_gain, ln2_shift,
               ch_w1, ch_b1, ch_w2, ch_b2, group_ids, out_grad):
    f32 = jnp.float32
    bf16 = jnp.bfloat16
    tp = lax.axis_size("tp")
    dp = lax.axis_size("dp")
    held = block_in.shape[0]
    images = held // tp
    width = block_in.shape[2] // S
    full = width * tp
    t = lax.axis_index("tp")

    def whole_images(stored):
        got = lax.all_to_all(stored.reshape(tp, images, S * width), "tp", 0, 0, tiled=True)
        return got.reshape(tp, images, S, width).transpose(1, 2, 0, 3).reshape(images, S, full)

    def stored(values):
        parts = values.reshape(images, S, tp, width).transpose(2, 0, 1, 3).reshape(tp, images, S * width)
        return lax.all_to_all(parts, "tp", 0, 0, tiled=True).reshape(held, 1, S * width)

    rows = ch_w1.shape[0]
    shard = jnp.stack([ch_w1.astype(bf16), ch_w2.T.astype(bf16)])
    gathered = lax.all_gather(lax.all_gather(shard, "tp", axis=1), "dp", axis=2)
    gathered = gathered.reshape(2, tp, dp * rows, shard.shape[2])
    norms = lax.all_gather(jnp.stack([ln1_gain, ln1_shift, ln2_gain, ln2_shift]), "tp", axis=1, tiled=True)
    x = whole_images(block_in).astype(f32)
    dz_low = whole_images(out_grad)
    token_w1 = tok_w1.astype(bf16)
    token_w2 = tok_w2.astype(bf16)
    xhat, inv_x = normalised(x)
    mixed = (xhat * norms[0] + norms[1]).astype(bf16)
    pre = jnp.einsum("nsc,sk->nkc", mixed, token_w1, preferred_element_type=f32) + tok_b1[:, None]
    hidden, hidden_back = jax.vjp(jax.nn.gelu, pre)
    hidden = hidden.astype(bf16)
    u = x + jnp.einsum("nkc,ks->nsc", hidden, token_w2, preferred_element_type=f32) + tok_b2[:, None]
    uhat, inv_u = normalised(u)
    count = images * S
    hn = (uhat * norms[2] + norms[3]).astype(bf16).reshape(count, full)
    dz = dz_low.reshape(count, full)
    z = jnp.zeros((count, full), f32)
    dhn = jnp.zeros((count, full), f32)
    grads1, grads2, bias = [], [], []
    inner = shard.shape[2]
    for j in range(tp):
        q = jnp.dot(hn, gathered[0, j], preferred_element_type=f32) + ch_b1[j * inner : (j + 1) * inner]
        g, g_back = jax.vjp(jax.nn.gelu, q)
        g = g.astype(bf16)
        z = z + jnp.einsum("rh,ch->rc", g, gathered[1, j], preferred_element_type=f32)
        dg = jnp.dot(dz, gathered[1, j], preferred_element_type=f32)
        dq = g_back(dg)[0].astype(bf16)
        grads2.append(jnp.einsum("rc,rh->ch", dz, g, preferred_element_type=f32).astype(bf16))
        grads1.append(jnp.einsum("rc,rh->ch", hn, dq, preferred_element_type=f32).astype(bf16))
        bias.append(jnp.sum(dq.astype(f32), 0))
        dhn = dhn + jnp.einsum("rh,ch->rc", dq, gathered[0, j], preferred_element_type=f32)
    z = (z + ch_b2).astype(bf16).astype(f32).reshape(u.shape)
    block_out = stored((u + z).astype(bf16))
    dhn = dhn.reshape(u.shape)
    dz32 = dz_low.astype(f32)
    image_gain = jnp.sum(dhn * uhat, 1)
    image_shift = jnp.sum(dhn, 1)
    du = dz32 + norm_back(dhn * norms[2], uhat, inv_u)
    dp_low = du.astype(bf16)
    dh = jnp.einsum("nsc,ks->nkc", dp_low, token_w2, preferred_element_type=f32)
    d_tok_w2 = jnp.einsum("nkc,nsc->ks", hidden, dp_low, preferred_element_type=f32)
    d_tok_b2 = jnp.sum(dp_low.astype(f32), (0, 2))
    dpre = hidden_back(dh)[0].astype(bf16)
    d_tok_w1 = jnp.einsum("nsc,nkc->sk", mixed, dpre, preferred_element_type=f32)
    d_tok_b1 = jnp.sum(dpre.astype(f32), (0, 2))
    da = jnp.einsum("nkc,sk->nsc", dpre, token_w1, preferred_element_type=f32)
    d_gain1 = jnp.sum(da * xhat, (0, 1))
    d_shift1 = jnp.sum(da, (0, 1))
    dx = stored((du + norm_back(da * norms[0], xhat, inv_x)).astype(bf16))

    gradient = jnp.stack([jnp.stack(grads1), jnp.stack(grads2)]).reshape(2, tp, dp, rows, inner)
    owned = lax.psum_scatter(lax.psum_scatter(gradient, "tp", scatter_dimension=1, tiled=True).astype(bf16), "dp", scatter_dimension=2, tiled=True)
    owned = owned.astype(f32).reshape(2, rows, inner)

    ids = lax.dynamic_slice_in_dim(group_ids, t * images, images)
    member = (ids[:, None] == jnp.arange(GROUPS)[None, :]).astype(f32)
    groups = jnp.dot(member.T, jnp.concatenate([image_gain, image_shift], 1), precision=highest)
    flat = [d_tok_w1, d_tok_w2, jnp.stack(bias), jnp.sum(dz32, (0, 1)), d_gain1, d_shift1, d_tok_b1, d_tok_b2, groups]
    sizes = [v.size for v in flat]
    need = sum(sizes)
    unit = 64 * full
    padded = -(-need // unit) * unit
    packed = jnp.concatenate([v.reshape(-1) for v in flat] + [jnp.zeros((padded - need,), f32)]).reshape(-1, full)
    total = lax.psum(packed, ("dp", "tp"))
    total = total.reshape(-1)
    pieces, start = [], 0
    for v in flat:
        pieces.append(total[start : start + v.size].reshape(v.shape))
        start += v.size
    tw1, tw2, cb1, cb2, g1, s1, tb1, tb2, gg = pieces
    gg = gg.reshape(GROUPS, 2, full)
    group_norms = jnp.sqrt(jnp.sum(gg * gg, (1, 2)))
    bound = 2.0 * math.sqrt(held * dp * S * full / GROUPS)
    factor = bound / jnp.maximum(group_norms, bound)
    clipped = jnp.sum(factor[:, None, None] * gg, 0)

    def mine(v):
        return lax.dynamic_slice_in_dim(v, t * width, width)

    return (block_out, dx, group_norms, mine(g1), mine(s1), tw1, tb1, tw2, tb2, mine(clipped[0]), mine(clipped[1]),
            owned[0], cb1.reshape(-1), owned[1].T, cb2)


def blocked(block_in, ln1_gain, ln1_shift, tok_w1, tok_b1, tok_w2, tok_b2, ln2_gain, ln2_shift,
            ch_w1, ch_b1, ch_w2, ch_b2, group_ids, out_grad):
    t = lax.axis_index("tp")
    held = block_in.shape[0]
    shard = jnp.stack([ch_w1.astype(BF16), ch_w2.T.astype(BF16)])
    xs, ds = block_in.reshape(4, 4 * HALF, 384), out_grad.reshape(4, 4 * HALF, 384)
    lnp = jnp.zeros((8, 4, 192), F32).at[:4, t].set(jnp.stack([ln1_gain, ln1_shift, ln2_gain, ln2_shift])).reshape(8, 768)
    w1, w2 = halves(tok_w1, 0).astype(BF16), halves(tok_w2, 1).astype(BF16)
    w, g, s, u, hn, x, dz, h, ts, op, norms = forward_pass(
        shard, xs, ds, lnp, w1.T, w2.T, tok_b1[:, None], halves(tok_b2, 0)[:, None], ch_b1.reshape(4, 1, 768), ch_b2[None])
    ids = lax.dynamic_slice_in_dim(group_ids, t * 4, 4)
    member = (ids[:, None] == jnp.arange(GROUPS)[None, :]).astype(F32)[:, :, None]
    bound = 2.0 * math.sqrt(held * 8 * S * 768 / GROUPS)
    out, dx, owned, total, fin, sizes = backward_pass(bound, w, g, s, u, hn, x, dz, h, ts, op, norms, w1, w2, member)
    own = lax.dynamic_index_in_dim(fin.reshape(8, 4, 192), t, 1, keepdims=False)
    tw1, tw2 = whole(total[:ROWS, :384], 0), whole(total[:ROWS, 384:], 0).T
    cb1 = total[HALF + 1 : HALF + 5].reshape(-1)
    tb2 = whole(total[204, :ROWS], 0)
    return (out.reshape(block_in.shape), dx.reshape(block_in.shape), sizes.reshape(-1), own[0], own[1], tw1, total[HALF, :384], tw2, tb2,
            own[2], own[3], owned[0], cb1, owned[1].T, total[205])


def solution(mesh):
    stored, own, copied = P("dp", "tp", None), P("tp"), P()
    in_specs = (stored, own, own, copied, copied, copied, copied, own, own, P("dp", "tp"), copied, P("tp", "dp"), copied, P("dp"), stored)
    out_specs = (stored, stored, copied, own, own, copied, copied, copied, copied, own, own, P("dp", "tp"), copied, P("tp", "dp"), copied)
    step = blocked if (mesh.shape["dp"], mesh.shape["tp"]) == (8, 4) else general
    return jax.shard_map(step, mesh=mesh, in_specs=in_specs, out_specs=out_specs, check_vma=False)
```

profile of v0, /device:TPU:0, one launch (start us, length us, event | category | flops | bytes accessed | tf_op | source)
XLA Modules:
  0.0 240.7 jit_solution(8649549658268527239)
XLA Ops:
  0.6 1.4 and_reduce_fusion
  2.0 1.4 broadcast_select_fusion
  3.5 0.7 reshape.204.lnp
  4.2 1.0 convert.26
  5.1 0.0 copy-start.5
  5.2 0.2 reshape.217
  5.3 0.2 fusion.11
  5.6 0.7 fusion.5
  6.3 0.8 copy.47.w1t
  7.1 0.0 copy-start.12
  7.1 0.2 reshape.218
  7.3 0.0 copy-start
  7.3 0.2 fusion.10
  7.5 0.2 copy.56
  7.7 0.2 copy.57
  7.9 0.8 fusion.4
  8.7 0.8 copy.48.w2t
  9.5 0.1 reshape.207
  9.6 0.2 slice_reduce_fusion.1
  9.8 0.1 fusion.7
  9.9 0.8 copy.50.b2
  10.7 2.7 %reshape.202.xs = bf16[4,392,384]{2,1,0:T(8,128)(2,1)} reshape(bf16[16,1,37632]{2,0,1:T(8,128)(2,1)S(1)} %copy-done) | data formatting | bytes 2408448 | tf_op jit(solution)/shard_map/reshape | solution.py:747
  13.3 2.7 %reshape.203.ds = bf16[4,392,384]{2,1,0:T(8,128)(2,1)} reshape(bf16[16,1,37632]{2,0,1:T(8,128)(2,1)S(1)} %copy-done.1) | data formatting | bytes 2408448 | tf_op jit(solution)/shard_map/reshape | solution.py:747
  16.1 0.7 pad_maximum_fusion.2.shard
  16.8 0.8 broadcast_in_dim.23.b1
  17.6 0.6 broadcast_in_dim.22.cb2
  18.2 89.3 %shard_map.262 = (bf16[2,4,8,96,768]{4,3,2,1,0:T(8,128)(2,1)}, bf16[4,4,208,768]{3,2,1,0:T(8,128)(2,1)}, bf16[4,4,208,768]{3,2,1,0:T(8,128)(2,1)}, f32[4,208,768...) custom-call(bf16[2,96,768]{2,1,0:T(8,128)(2,1)} %pad_maximum_fusion., ...), custom_call_target="tpu_custom_call" | custom-call | tf_op jit(solution)/shard_map/pallas_call | solution.py:331
  107.5 0.1 dynamic_slice.7
  107.6 0.7 fusion.6.member
  108.3 116.6 %shard_map.263 = (bf16[4,392,384]{2,1,0:T(8,128)(2,1)}, bf16[4,392,384]{2,1,0:T(8,128)(2,1)}, f32[2,96,768]{2,1,0:T(8,128)}, f32[384,768]{1,0:T(8,128)}, f32[8,768]{1,0:T(8,128)}, /*index=5*/f32[64,1]{1,0:T(8,128)}) custom-call(bf16[2,4,8,96,768]{4,3,2,1,0:T(8,128)(2,1)} %get-tuple-element.44.w_in, bf16[4,4,208,768]{3,2,1,0:T(8,128)(2,1)} %get-tuple-element.45.g_in, ...), custom_call_target="tpu_custom_call" | custom-call | tf_op jit(solution)/shard_map/pallas_call | solution.py:591
  224.9 0.8 slice_bitcast_fusion.7
  225.8 0.1 copy.53
  225.9 0.7 reshape.215
  226.6 1.2 slice_bitcast_fusion.3
  227.8 0.2 copy.52
  228.0 0.9 reshape.214
  228.9 0.2 copy.51
  229.1 0.9 reshape.213
  230.0 2.3 reshape.209
  232.3 2.3 reshape.210
  234.6 0.8 slice_bitcast_fusion
  235.4 0.1 reshape.212
  235.5 0.6 constant_dynamic-slice_fusion.3
  236.1 0.7 slice.124
  236.9 0.6 reshape.216
  237.5 1.3 slice_reduce_fusion.2
  238.8 1.3 slice_reduce_fusion.3
  240.1 0.6 reduce.9
  (34 shorter events, 0.3 us)
Async XLA Ops:
  5.1 1.9 copy-start.5
  7.1 2.4 copy-start.12
  7.3 3.4 %copy-start = (bf16[16,1,37632]{2,0,1:T(8,128)(2,1)S(1)}, bf16[16,1,37632]{2,0,1:T(8,128)(2,1)}, u32[]{:S(2)}) copy-start(bf16[16,1,37632]{2,0,1:T(8,128)(2,1)} %param.17) | copy-start | bytes 3612676
  10.7 2.7 %copy-start.1 = (bf16[16,1,37632]{2,0,1:T(8,128)(2,1)S(1)}, bf16[16,1,37632]{2,0,1:T(8,128)(2,1)}, u32[]{:S(2)}) copy-start(bf16[16,1,37632]{2,0,1:T(8,128)(2,1)} %param.31) | copy-start | bytes 3612676
  13.3 2.7 %copy-start.6 = (f32[768,96]{0,1:T(8,128)S(1)}, f32[768,96]{0,1:T(8,128)}, u32[]{:S(2)}) copy-start(f32[768,96]{0,1:T(8,128)} %param.28) | copy-start | bytes 884740
  13.3 2.7 %copy-start.7 = (f32[96,768]{1,0:T(8,128)S(1)}, f32[96,768]{1,0:T(8,128)}, u32[]{:S(2)}) copy-start(f32[96,768]{1,0:T(8,128)} %param.26) | copy-start | bytes 884740
  16.0 0.8 copy-start.11
  16.0 1.6 copy-start.10
  18.2 89.3 %copy-start.13 = (s32[16]{0:T(128)S(1)}, s32[16]{0:T(128)}, u32[]{:S(2)}) copy-start(s32[16]{0:T(128)} %param.30) | copy-start | bytes 196
  228.0 2.1 copy-start.3
  230.0 2.3 copy-start.2
  232.3 2.3 copy-start.4
  232.3 3.1 %copy-start.9 = (f32[8,768]{1,0:T(8,128)S(1)}, f32[8,768]{1,0:T(8,128)}, u32[]{:S(2)}) copy-start(f32[8,768]{1,0:T(8,128)} %get-tuple-element.58) | copy-start | bytes 73732
  234.6 5.5 %copy-start.8 = (f32[64,1]{1,0:T(8,128)S(1)}, f32[64,1]{1,0:T(8,128)}, u32[]{:S(2)}) copy-start(f32[64,1]{1,0:T(8,128)} %get-tuple-element.57) | copy-start | bytes 772
where the time goes:
time: 241 us
  Pallas kernels  206 us (85%)
  local copies, waits for them, and re-layouts  26.5 us (11%)
  other arithmetic  7.55 us (3%)
    pallas_call x1, Pallas kernels, backward_pass(): pl.pallas_call(functools.partial(backward_kernel, bound), out_shape=[sds(...  117 us
    pallas_call x1, Pallas kernels, forward_pass(): pl.pallas_call(forward_kernel, out_shape=[sds(*v) for v in shapes], in_sp...  89.3 us

commit v1 on v0

v1 whole, which is shorter than its diff:
```python
import functools
import math

import jax
import jax.numpy as jnp
from jax import lax
from jax.experimental import pallas as pl
from jax.experimental.pallas import tpu as pltpu
from jax.sharding import PartitionSpec as P

MESH = pl.DeviceIdType.MESH


S = 196
GROUPS = 64
F32 = jnp.float32
BF16 = jnp.bfloat16
HALF = 98
GAP = 104
ROWS = 208
BLOCK = 4 * HALF
LOW = math.sqrt(2.0 / math.pi)
CUBE = 0.044715


def place():
    dp = lax.axis_index("dp")
    t = lax.axis_index("tp")
    c, x, y = dp % 2, (dp // 2) % 2, dp // 4
    near = dict(S=owner(y, x, 1 - c), X=owner(y, 1 - x, c), Y=owner(1 - y, x, c), D=owner(1 - y, 1 - x, c))
    return dp, t, near, (y, x, c)


def owner(y, x, c):
    return (y * 2 + x) * 2 + c


def others(t):
    first = jnp.where(t == 0, 1, jnp.where(t == 1, 0, jnp.where(t == 2, 3, 2)))
    second = jnp.where(t == 0, 2, jnp.where(t == 1, 2, 1))
    third = jnp.where(t < 2, 3, 0)
    return [first, second, third]


def meet(devices):
    barrier = pltpu.get_barrier_semaphore()
    for device in devices:
        pl.semaphore_signal(barrier, inc=1, device_id=device, device_id_type=MESH)
    pl.semaphore_wait(barrier, len(devices))


def remote(src, dst, ss, rs, device):
    return pltpu.make_async_remote_copy(src_ref=src, dst_ref=dst, send_sem=ss, recv_sem=rs, device_id=device, device_id_type=MESH)


def gelu_pair(v):
    square = v * v
    up = 0.5 * jnp.tanh(v * (LOW + (LOW * CUBE) * square)) + 0.5
    value = v * up
    slope = up + value * (1.0 - up) * (2.0 * LOW + (6.0 * LOW * CUBE) * square)
    return value, slope


def turn(v):
    return pltpu.roll(v, 64, 1)


def lane_low():
    return lax.broadcasted_iota(jnp.int32, (HALF, 128), 1) < 64


def join_groups(flat, image, store):
    low = lane_low()
    for p in range(2):
        a = [flat[j, pl.ds(2 * p * BLOCK + image * HALF, HALF), :] for j in range(3)]
        b = [flat[j, pl.ds((2 * p + 1) * BLOCK + image * HALF, HALF), :] for j in range(3)]
        a1, a2, b0, b1 = turn(a[1]), turn(a[2]), turn(b[0]), turn(b[1])
        even = [a[0], jnp.where(low, a[1], b0), jnp.where(low, b0, b1)]
        odd = [jnp.where(low, a1, a2), jnp.where(low, a2, b[1]), b[2]]
        for j in range(3):
            store(0, 384 * p + 128 * j, even[j])
            store(GAP, 384 * p + 128 * j, odd[j])


def split_groups(load, flat, image):
    low = lane_low()
    for p in range(2):
        e = [load(0, 384 * p + 128 * j) for j in range(3)]
        o = [load(GAP, 384 * p + 128 * j) for j in range(3)]
        e1, e2, o0, o1 = turn(e[1]), turn(e[2]), turn(o[0]), turn(o[1])
        a = [e[0], jnp.where(low, e[1], o0), jnp.where(low, o0, o1)]
        b = [jnp.where(low, e1, e2), jnp.where(low, e2, o[1]), o[2]]
        for j in range(3):
            flat[j, pl.ds(2 * p * BLOCK + image * HALF, HALF), :] = a[j]
            flat[j, pl.ds((2 * p + 1) * BLOCK + image * HALF, HALF), :] = b[j]


def spread(packed, flat):
    for k in range(4):
        for j in range(3):
            flat[j, pl.ds(k * BLOCK, BLOCK), :] = packed[k, :, 128 * j : 128 * j + 128].astype(F32)


def pack(flat, packed):
    for k in range(4):
        for j in range(3):
            packed[k, :, 128 * j : 128 * j + 128] = flat[j, pl.ds(k * BLOCK, BLOCK), :].astype(BF16)


def to_rows(stored, flat):
    for i in range(HALF):
        for j in range(3):
            start = 384 * i + 128 * j
            flat[j, pl.ds(i, 16, stride=HALF), :] = stored[:, start : start + 128].astype(F32)


def to_stored(flat, stored):
    for i in range(HALF):
        for j in range(3):
            start = 384 * i + 128 * j
            stored[:, start : start + 128] = flat[j, pl.ds(i, 16, stride=HALF), :].astype(BF16)


def hat(v):
    average = jnp.mean(v, -1, keepdims=True)
    inverse = lax.rsqrt(jnp.mean(v * v, -1, keepdims=True) - average * average + 1e-06)
    return (v - average) * inverse, inverse


def dot(a, b):
    return jnp.dot(a, b, preferred_element_type=F32)


def dot_nt(a, b):
    return lax.dot_general(a, b, (((1,), (1,)), ((), ())), preferred_element_type=F32)


def forward_kernel(cw1, cw2, xin, din, p0, p1, p2, p3, tw1, tw2, b1, b2, cb1, cb2,
                   w_out, g_out, s_out, u_out, hn_out, x_out, dz_out, h_out, t_out, o_out, ln_out, w1_out, w2_out,
                   wf, shard, wv, stored, xs, ds, xr, dr, flat, x, xb, u, hn, hnt, g, s, h, ts, zs, op, dz, lr, lall, t3, c2, w1, w2, w1t, w2t,
                   send_sem, recv_sem, line_sem, x_send, x_recv, d_send, d_recv, l_send, l_recv, in_sem, keep_sem):
    dp, t, near, (y, xx, c) = place()
    line = others(t)
    order = [t] + line
    started, kept, maybe = [], [], []

    def go(copy):
        copy.start()
        started.append(copy)

    def keep(src, dst):
        copy = pltpu.make_async_copy(src, dst, keep_sem.at[len(kept)])
        copy.start()
        kept.append(copy)

    def bring(src, dst, n):
        copy = pltpu.make_async_copy(src, dst, in_sem.at[n])
        copy.start()
        return copy

    in_w1, in_w2 = bring(cw1, wf.at[0], 0), bring(cw2, wf.at[1], 1)
    in_x, in_d = bring(xin, stored.at[0], 2), bring(din, stored.at[1], 3)
    meet([(near["S"], t), (near["X"], t), (near["Y"], t)] + [(dp, p) for p in line])
    sends = [0]

    def send(src, who, tt, device):
        go(remote(src, wv.at[:, tt, who], send_sem.at[sends[0]], recv_sem.at[who, tt], device))
        sends[0] += 1

    def along(src, tt, target):
        n = len(maybe)
        inside = (target >= 0) & (target <= 3)
        copy = remote(src, wv.at[:, tt, dp], line_sem.at[n], recv_sem.at[dp, tt], (dp, jnp.clip(target, 0, 3)))
        pl.when(inside)(copy.start)
        maybe.append((inside, copy))

    def arrived(who, tt):
        ref = wv.at[:, tt, who]
        remote(ref, ref, send_sem.at[0], recv_sem.at[who, tt], (dp, t)).wait_recv()

    in_w1.wait()
    in_w2.wait()
    shard[...] = wf[...].astype(BF16)
    along(shard, t, t + 1)
    along(shard, t, t - 1)
    for name in "XYS":
        send(shard, dp, t, (near[name], t))
    wv[:, t, dp] = shard[...]
    for n, ref in enumerate((p0, p1, p2, p3)):
        row = ref[...].reshape(1, 192)
        wide = jnp.concatenate([row, row, row, row], 1)
        lane = lax.broadcasted_iota(jnp.int32, (1, 768), 1)
        lr[t, n : n + 1, :] = jnp.where((lane >= 192 * t) & (lane < 192 * t + 192), wide, 0.0)
    for n, p in enumerate(line):
        go(remote(lr.at[t], lr.at[t], l_send.at[n], l_recv.at[t], (dp, p)))

    def column(k):
        tt = order[k]
        arrived(dp, tt)
        src = wv.at[:, tt, dp]
        along(src, tt, jnp.where(tt < t, t + 1, t - 1))
        for name in "XYS":
            send(src, dp, tt, (near[name], t))

    def neighbours(k):
        tt = order[k]
        first, second = ("X", "Y") if k % 2 == 0 else ("Y", "X")
        arrived(near[first], tt)
        src = wv.at[:, tt, near[first]]
        send(src, near[first], tt, (near[second], t))
        send(src, near[first], tt, (near["S"], t))
        arrived(near[second], tt)
        send(wv.at[:, tt, near[second]], near[second], tt, (near["S"], t))

    def diagonal(k):
        tt = order[k]
        arrived(near["D"], tt)
        send(wv.at[:, tt, near["D"]], near["D"], tt, (near["S"], t))

    def exchange(src, dst, ss, rs):
        for n, p in enumerate(line):
            go(remote(src.at[p], dst.at[t], ss.at[n], rs.at[t], (dp, p)))

    in_x.wait()
    to_rows(stored.at[0], flat)
    pack(flat, xs)
    column(1)
    neighbours(0)
    column(2)
    exchange(xs, xr, x_send, x_recv)
    xr[t] = xs[t]
    neighbours(1)
    diagonal(0)
    column(3)
    in_d.wait()
    to_rows(stored.at[1], flat)
    pack(flat, ds)
    dr[t] = ds[t]
    gap = jnp.zeros((GAP - HALF, 128), F32)
    for n, (src, dst) in enumerate(((tw1, w1), (tw2, w2t))):
        for j in range(3):
            t3[j] = src[:, 128 * j : 128 * j + 128]
        for j in range(3):
            even, odd = t3[j, pl.ds(0, HALF, stride=2), :], t3[j, pl.ds(1, HALF, stride=2), :]
            dst[:, 128 * j : 128 * j + 128] = jnp.concatenate([even, gap, odd, gap], 0).astype(BF16)
    w1t[...] = w1[...].T
    w2[...] = w2t[...].T
    keep(w1, w1_out)
    keep(w2, w2_out)
    c2[...] = jnp.broadcast_to(b2[...].reshape(1, S), (128, S)).T
    few = jnp.zeros((GAP - HALF, 1), F32)
    shift2 = jnp.concatenate([c2[pl.ds(0, HALF, stride=2), :][:, 0:1], few, c2[pl.ds(1, HALF, stride=2), :][:, 0:1], few], 0)
    shift1 = jnp.broadcast_to(b1[...].reshape(1, 384), (8, 384)).T[:, 0:1]
    neighbours(2)
    diagonal(1)
    neighbours(3)
    diagonal(2)
    diagonal(3)

    for p in line:
        remote(lr.at[p], lr.at[p], l_send.at[0], l_recv.at[p], (dp, t)).wait_recv()
    params = (lr[0] + lr[1]) + (lr[2] + lr[3])
    lall[...] = params
    keep(lall, ln_out)
    zero = jnp.zeros((GAP - HALF, 768), F32)
    for n in range(4):
        for start in (HALF, GAP + HALF):
            x[n, start : start + GAP - HALF, :] = zero
    for p in line:
        remote(xr.at[p], xr.at[p], x_send.at[0], x_recv.at[p], (dp, t)).wait_recv()
    exchange(ds, dr, d_send, d_recv)
    spread(xr, flat)
    for n in range(4):
        def put(row, lane, v, n=n):
            x[n, row : row + HALF, lane : lane + 128] = v
        join_groups(flat, n, put)
        xb[n] = x[n].astype(BF16)
    keep(xb, x_out)
    g1, s1, g2, s2 = params[0:1], params[1:2], params[2:3], params[3:4]

    def token(n, carry):
        v = x[n]
        xhat, _ = hat(v)
        a = (xhat * g1 + s1).astype(BF16)
        value, slope = gelu_pair(dot(w1t[...], a) + shift1)
        low = value.astype(BF16)
        h[n] = low
        ts[n] = slope.astype(BF16)
        r = v + dot(w2t[...], low) + shift2
        u[n] = r
        uhat, _ = hat(r)
        hn[n] = (uhat * g2 + s2).astype(BF16)
        return carry

    lax.fori_loop(0, 4, token, 0)
    keep(u, u_out)
    keep(h, h_out)
    keep(ts, t_out)

    for k in range(4):
        tt = order[k]
        for yy, xxx in ((y, xx), (y, 1 - xx), (1 - y, xx), (1 - y, 1 - xx)):
            arrived(owner(yy, xxx, 1 - c), tt)
        keep(wv.at[:, tt], w_out.at[:, tt])

        def block(n, carry, tt=tt, k=k):
            value, slope = gelu_pair(dot(hn[n], wv[0, tt].reshape(768, 768)) + cb1[pl.ds(pl.multiple_of(tt * 768, 128), 768)].reshape(1, 768))
            low = value.astype(BF16)
            g[tt, n] = low
            s[tt, n] = slope.astype(BF16)
            part = dot_nt(low, wv[1, tt].reshape(768, 768))
            if k == 0:
                zs[n] = part
            elif k < 3:
                zs[n] += part
            else:
                z = (zs[n] + part + cb2[...].reshape(1, 768)).astype(BF16).astype(F32)
                zs[n] = u[n] + z
            return carry

        lax.fori_loop(0, 4, block, 0)
        keep(g.at[tt], g_out.at[tt])
        keep(s.at[tt], s_out.at[tt])
    for n in range(4):
        split_groups(lambda row, lane, n=n: zs[n, row : row + HALF, lane : lane + 128], flat, n)
    pack(flat, op)
    keep(op, o_out)
    for n in range(4):
        hnt[:, n * ROWS : (n + 1) * ROWS] = hn[n].T
    keep(hnt, hn_out)
    for p in line:
        remote(dr.at[p], dr.at[p], d_send.at[0], d_recv.at[p], (dp, t)).wait_recv()
    spread(dr, flat)
    for n in range(4):
        for start in (HALF, GAP + HALF):
            zs[n, start : start + GAP - HALF, :] = zero

        def put_grad(row, lane, v, n=n):
            zs[n, row : row + HALF, lane : lane + 128] = v

        join_groups(flat, n, put_grad)
        dz[n] = zs[n].astype(BF16)
    keep(dz, dz_out)
    for copy in started:
        copy.wait_send()
    for inside, copy in maybe:
        pl.when(inside)(copy.wait_send)
    for copy in kept:
        copy.wait()


def forward_pass(*operands):
    any_, vmem = pl.BlockSpec(memory_space=pl.ANY), pl.BlockSpec(memory_space=pltpu.VMEM)
    sds = jax.ShapeDtypeStruct
    dma = pltpu.SemaphoreType.DMA
    wshape, act, tok, packed = (2, 4, 8, 96, 768), (4, ROWS, 768), (4, 384, 768), (4, BLOCK, 384)
    shapes = [(wshape, BF16), ((4,) + act, BF16), ((4,) + act, BF16), (act, F32), ((768, 4 * ROWS), BF16), (act, BF16), (act, BF16),
              (tok, BF16), (tok, BF16), (packed, BF16), ((8, 768), F32), ((ROWS, 384), BF16), ((384, ROWS), BF16)]
    V = pltpu.VMEM
    return pl.pallas_call(forward_kernel,
        out_shape=[sds(*v) for v in shapes],
        in_specs=[any_] * 4 + [vmem] * 10, out_specs=[any_] * len(shapes),
        scratch_shapes=[V((2, 96, 768), F32), V((2, 96, 768), BF16), V(wshape, BF16), V((2, 16, HALF * 384), BF16), V(packed, BF16), V(packed, BF16),
            V(packed, BF16), V(packed, BF16), V((3, 4 * BLOCK, 128), F32), V(act, F32), V(act, BF16), V(act, F32), V(act, BF16), V((768, 4 * ROWS), BF16),
            V((4,) + act, BF16), V((4,) + act, BF16), V(tok, BF16), V(tok, BF16), V(act, F32), V(packed, BF16), V(act, BF16), V((4, 8, 768), F32), V((8, 768), F32),
            V((3, S, 128), F32), V((S, 128), F32), V((ROWS, 384), BF16), V((384, ROWS), BF16), V((384, ROWS), BF16), V((ROWS, 384), BF16),
            dma((28,)), dma((8, 4)), dma((5,)), dma((3,)), dma((4,)), dma((3,)), dma((4,)), dma((3,)), dma((4,)), dma((4,)), dma((24,))],
        compiler_params=pltpu.CompilerParams(collective_id=1, has_side_effects=True, vmem_limit_bytes=60 << 20))(*operands)


PIECE = 48
SMALL = 8 * PIECE


def backward_kernel(w_in, g_in, s_in, u_in, hn_in, x_in, dz_in, h_in, t_in, op, norms, w1, w2, ids,
                    o_out, dx_out, w_grad, total_out,
                    wv, g, s, u, x, dz, h, ts, hnt, dzt, dhn, gr, flat, dxp,
                    sib, first, second, final, zbuf, small, t_sib, t_chip, t_line, t_full,
                    load_sem, slot_sem, own_sem, o_send, o_recv, x_send, x_recv, sib_sem, sib_recv, a_send, a_recv, z_send, z_recv,
                    p_send, p_recv, c_send, c_recv, l_send, l_recv, m_send, m_recv, b_send, b_recv, e_send, e_recv):
    dp, t, near, (y, xx, c) = place()
    line = others(t)
    order = [line[2], line[1], line[0], t]
    chips = {"O": (y, xx), "X": (y, 1 - xx), "Y": (1 - y, xx), "D": (1 - y, 1 - xx)}
    slot = {"O": 0, "X": 1, "Y": 2, "D": 3}
    started = []

    def go(copy):
        copy.start()
        started.append(copy)

    def load(src, dst, sem):
        copy = pltpu.make_async_copy(src, dst, sem)
        copy.start()
        return copy

    def fetch(k):
        return load(w_in.at[:, order[k]], wv.at[k % 2], slot_sem.at[k % 2])

    load_dz = load(dz_in, dz, load_sem.at[0])
    load_g = [load(g_in.at[order[k]], g.at[k], load_sem.at[1 + k]) for k in range(4)]
    slots = {0: fetch(0), 1: fetch(1)}
    load_s = [load(s_in.at[order[k]], s.at[k], load_sem.at[5 + k]) for k in range(4)]
    later = [load(u_in, u, load_sem.at[9]), load(x_in, x, load_sem.at[10]), load(h_in, h, load_sem.at[11]), load(t_in, ts, load_sem.at[12])]
    load_hn = load(hn_in, hnt, load_sem.at[13])
    meet([(near["S"], t), (near["X"], t), (near["Y"], t), (near["D"], t)] + [(dp, p) for p in line])
    own_o = load(op.at[t], o_out.at[t], own_sem.at[0])
    for n, p in enumerate(line):
        go(remote(op.at[p], o_out.at[t], o_send.at[n], o_recv.at[t], (dp, p)))

    def hand_over(j, k):
        for name in "DXYO":
            n = slot[name]
            go(remote(gr.at[j, k, owner(*chips[name], 1 - c)], sib.at[j, k, n], sib_sem.at[j, k, n], sib_recv.at[j, k, n], (near["S"], t)))

    def chip_sum(j, k, name):
        n = slot[name]
        remote(sib.at[j, k, n], sib.at[j, k, n], sib_sem.at[j, k, n], sib_recv.at[j, k, n], (near["S"], t)).wait_recv()
        sib[j, k, n] = (gr[j, k, owner(*chips[name], c)].astype(F32) + sib[j, k, n].astype(F32)).astype(BF16)

    def ways(k):
        return ("X", "Y") if k % 2 == 0 else ("Y", "X")

    def hop(j, k, src, dst, n, name):
        go(remote(src, dst, a_send.at[j, k, n], a_recv.at[j, k, n], (near[name], t)))

    def landed(j, k, dst, n):
        remote(dst, dst, a_send.at[j, k, n], a_recv.at[j, k, n], (near["S"], t)).wait_recv()

    def stage_one(j, k):
        f, s2 = ways(k)
        chip_sum(j, k, "D")
        hop(j, k, sib.at[j, k, 3], first.at[j, k], 0, s2)
        chip_sum(j, k, s2)
        hop(j, k, sib.at[j, k, slot[s2]], second.at[j, k], 1, s2)

    def stage_two(j, k):
        f, s2 = ways(k)
        n = slot[f]
        chip_sum(j, k, f)
        landed(j, k, first.at[j, k], 0)
        sib[j, k, n] = (sib[j, k, n].astype(F32) + first[j, k].astype(F32)).astype(BF16)
        hop(j, k, sib.at[j, k, n], final.at[j, k], 2, f)

    def stage_three(j, k):
        chip_sum(j, k, "O")
        landed(j, k, second.at[j, k], 1)
        landed(j, k, final.at[j, k], 2)
        total = sib[j, k, 0].astype(F32) + second[j, k].astype(F32) + final[j, k].astype(F32)
        if k < 3:
            sib[j, k, 0] = total.astype(BF16)
            go(remote(sib.at[j, k, 0], zbuf.at[j, t], z_send.at[j, k], z_recv.at[j, t], (dp, order[k])))
        else:
            w_grad[j] = total

    zero = jnp.zeros((1, 768), F32)
    load_dz.wait()
    for n in range(4):
        dzt[:, n * ROWS : (n + 1) * ROWS] = dz[n].T

    def second_weight(k):
        load_g[k].wait()
        gr[1, k] = dot(dzt[...], g[k].reshape(4 * ROWS, 768)).astype(BF16).reshape(8, 96, 768)
        hand_over(1, k)

    def data(k):
        n2 = k % 2
        slots[k].wait()
        load_s[k].wait()

        def image(n, bias):
            low = (dot(dz[n], wv[n2, 1].reshape(768, 768)) * s[k, n].astype(F32)).astype(BF16)
            s[k, n] = low
            part = dot_nt(low, wv[n2, 0].reshape(768, 768))
            if k == 0:
                dhn[n] = part
            else:
                dhn[n] += part
            return bias + jnp.sum(low.astype(F32), 0, keepdims=True)

        bias = lax.fori_loop(0, 4, image, zero)
        small[pl.ds(HALF + 1 + order[k], 1), :] = bias
        if k < 2:
            slots[k + 2] = fetch(k + 2)

    def first_weight(k):
        gr[0, k] = dot(hnt[...], s[k].reshape(4 * ROWS, 768)).astype(BF16).reshape(8, 96, 768)
        hand_over(0, k)

    g1, s1, g2 = norms[0:1], norms[1:2], norms[2:3]
    row = lax.broadcasted_iota(jnp.int32, (ROWS, 768), 0)
    ones = jnp.ones((8, 768), BF16)
    groups = lax.broadcasted_iota(jnp.int32, (GROUPS, 16), 0) == ids[...].reshape(1, 16)
    lane = lax.broadcasted_iota(jnp.int32, (GROUPS, 16), 1)

    def token(n, carry):
        sum_g1, sum_s1, sum_b2 = carry
        d, grad = dhn[n], dz[n].astype(F32)
        uhat, inv_u = hat(u[n])
        member = jnp.sum(jnp.where(groups & (lane == 4 * t + n), 1.0, 0.0), -1, keepdims=True)
        small[208:272, :] += member * jnp.sum(d * uhat, 0, keepdims=True)
        small[272:336, :] += member * jnp.sum(d, 0, keepdims=True)
        e = d * g2
        du = grad + inv_u * (e - jnp.mean(e, -1, keepdims=True) - uhat * jnp.mean(e * uhat, -1, keepdims=True))
        low = du.astype(BF16)
        dpre = (dot(w2[...], low) * ts[n].astype(F32)).astype(BF16)
        xhat, inv_x = hat(x[n].astype(F32))
        a = jnp.where(row == HALF, 1.0, xhat * g1 + s1).astype(BF16)
        tok1 = dot_nt(a, dpre)
        tok2 = dot_nt(low, h[n])
        for start, size in ((0, HALF + 1), (GAP, HALF)):
            small[start : start + size, 0:384] += tok1[start : start + size]
        for start, size in ((0, HALF), (GAP, HALF)):
            small[start : start + size, 384:768] += tok2[start : start + size]
        da = dot(w1[...], dpre)
        e1 = da * g1
        dhn[n] = du + inv_x * (e1 - jnp.mean(e1, -1, keepdims=True) - xhat * jnp.mean(e1 * xhat, -1, keepdims=True))
        return (sum_g1 + jnp.sum(da * xhat, 0, keepdims=True), sum_s1 + jnp.sum(da, 0, keepdims=True), sum_b2 + dot_nt(ones, low))

    small[...] = jnp.zeros((SMALL, 768), F32)
    second_weight(0)
    second_weight(1)
    stage_one(1, 0)
    second_weight(2)
    stage_one(1, 1)
    second_weight(3)
    stage_one(1, 2)
    stage_one(1, 3)
    data(0)
    stage_two(1, 0)
    stage_two(1, 1)
    data(1)
    stage_two(1, 2)
    stage_two(1, 3)
    data(2)
    stage_three(1, 0)
    stage_three(1, 1)
    data(3)
    stage_three(1, 2)
    stage_three(1, 3)
    for copy in later:
        copy.wait()
    carry = lax.fori_loop(0, 4, token, (zero, zero, jnp.zeros((8, ROWS), F32)))
    for n in range(4):
        split_groups(lambda r, lane, n=n: dhn[n, r : r + HALF, lane : lane + 128], flat, n)
    pack(flat, dxp)
    own_x = load(dxp.at[t], dx_out.at[t], own_sem.at[1])
    for n, p in enumerate(line):
        go(remote(dxp.at[p], dx_out.at[t], x_send.at[n], x_recv.at[t], (dp, p)))
    small[202:203, :] = carry[0]
    small[203:204, :] = carry[1]
    small[204:205, 0:ROWS] = carry[2][0:1]
    total_dz = zero
    for n in range(4):
        total_dz += jnp.sum(dz[n].astype(F32), 0, keepdims=True)
    small[205:206, :] = total_dz

    chip = dp // 2
    far = [("X", near["X"] // 2), ("Y", near["Y"] // 2), ("D", near["D"] // 2)]

    def part(ref, core, q):
        return ref.at[pl.ds(pl.multiple_of((core * 4 + q) * PIECE, 8), PIECE)]

    def half(ref, core):
        return ref.at[pl.ds(pl.multiple_of(core * 4 * PIECE, 8), 4 * PIECE)]

    def quarter(ref, p):
        return ref.at[pl.ds(pl.multiple_of((p // 2) * (PIECE // 2), 8), PIECE // 2), pl.ds(pl.multiple_of((p % 2) * 384, 128), 384)]

    go(remote(half(small, 1 - c), t_sib, p_send, p_recv, (near["S"], t)))
    load_hn.wait()
    first_weight(0)
    remote(t_sib, t_sib, p_send, p_recv, (near["S"], t)).wait_recv()
    half(small, c)[...] += t_sib[...]
    for n, (name, q) in enumerate(far):
        go(remote(part(small, c, q), t_chip.at[n], c_send.at[n], c_recv.at[n], (near[name], t)))
    first_weight(1)
    stage_one(0, 0)
    first_weight(2)
    stage_one(0, 1)
    first_weight(3)
    stage_one(0, 2)
    stage_one(0, 3)
    total = part(small, c, chip)[...]
    for n in range(3):
        remote(t_chip.at[n], t_chip.at[n], c_send.at[n], c_recv.at[n], (near["S"], t)).wait_recv()
        total = total + t_chip[n]
    t_full[...] = total
    for n, p in enumerate(line):
        go(remote(quarter(t_full, p), t_line.at[t], l_send.at[n], l_recv.at[t], (dp, p)))
    t_line[t] = quarter(t_full, t)[...]
    stage_two(0, 0)
    stage_two(0, 1)
    for p in line:
        remote(t_line.at[p], t_line.at[p], l_send.at[0], l_recv.at[p], (dp, t)).wait_recv()
    own = part(total_out, c, chip)
    mine = quarter(own, t)
    mine[...] = ((t_line[0] + t_line[1]) + t_line[2]) + t_line[3]
    for n, p in enumerate(line):
        go(remote(mine, mine, m_send.at[n], m_recv.at[t], (dp, p)))
    stage_two(0, 2)
    stage_two(0, 3)
    stage_three(0, 0)
    for p in line:
        there = quarter(own, p)
        remote(there, there, m_send.at[0], m_recv.at[p], (dp, t)).wait_recv()
    for n, (name, q) in enumerate(far):
        go(remote(own, own, b_send.at[n], b_recv.at[chip], (near[name], t)))
    go(remote(own, own, e_send.at[3], e_recv.at[chip], (near["S"], t)))
    stage_three(0, 1)
    stage_three(0, 2)
    stage_three(0, 3)
    for n, (name, q) in enumerate(far):
        there = part(total_out, c, q)
        remote(there, there, b_send.at[0], b_recv.at[q], (dp, t)).wait_recv()
        go(remote(there, there, e_send.at[n], e_recv.at[q], (near["S"], t)))
    for j in (1, 0):
        for p in line:
            remote(zbuf.at[j, p], zbuf.at[j, p], z_send.at[j, 0], z_recv.at[j, p], (dp, t)).wait_recv()
            w_grad[j] += zbuf[j, p].astype(F32)
    for q in range(4):
        there = part(total_out, 1 - c, q)
        remote(there, there, e_send.at[0], e_recv.at[q], (dp, t)).wait_recv()
    own_o.wait()
    own_x.wait()
    for p in line:
        remote(o_out.at[p], o_out.at[p], o_send.at[0], o_recv.at[p], (dp, t)).wait_recv()
        remote(dx_out.at[p], dx_out.at[p], x_send.at[0], x_recv.at[p], (dp, t)).wait_recv()
    for copy in started:
        copy.wait_send()


def backward_pass(*operands):
    any_, vmem = pl.BlockSpec(memory_space=pl.ANY), pl.BlockSpec(memory_space=pltpu.VMEM)
    sds = jax.ShapeDtypeStruct
    dma = pltpu.SemaphoreType.DMA
    V = pltpu.VMEM
    act, tok, packed, piece = (4, ROWS, 768), (4, 384, 768), (4, BLOCK, 384), (96, 768)
    return pl.pallas_call(backward_kernel,
        out_shape=[sds(packed, BF16), sds(packed, BF16), sds((2,) + piece, F32), sds((SMALL, 768), F32)],
        in_specs=[any_] * 10 + [vmem] * 4, out_specs=[any_] * 2 + [vmem] * 2,
        scratch_shapes=[V((2, 2, 8, 96, 768), BF16), V((4,) + act, BF16), V((4,) + act, BF16), V(act, F32), V(act, BF16), V(act, BF16),
            V(tok, BF16), V(tok, BF16), V((768, 4 * ROWS), BF16), V((768, 4 * ROWS), BF16), V(act, F32),
            V((2, 4, 8, 96, 768), BF16), V((3, 4 * BLOCK, 128), F32), V(packed, BF16),
            V((2, 4, 4) + piece, BF16), V((2, 4) + piece, BF16), V((2, 4) + piece, BF16), V((2, 4) + piece, BF16), V((2, 4) + piece, BF16),
            V((SMALL, 768), F32), V((4 * PIECE, 768), F32), V((3, PIECE, 768), F32), V((4, PIECE // 2, 384), F32), V((PIECE, 768), F32),
            dma((14,)), dma((2,)), dma((2,)), dma((3,)), dma((4,)), dma((3,)), dma((4,)), dma((2, 4, 4)), dma((2, 4, 4)), dma((2, 4, 3)), dma((2, 4, 3)),
            dma((2, 4)), dma((2, 4)), dma, dma, dma((3,)), dma((3,)), dma((3,)), dma((4,)), dma((3,)), dma((4,)), dma((3,)), dma((4,)), dma((4,)), dma((4,))],
        compiler_params=pltpu.CompilerParams(collective_id=2, has_side_effects=True, vmem_limit_bytes=62 << 20))(*operands)


def finish_kernel(bound, o, dx, grads, total, o_stored, dx_stored, d1, d2, tok1, tok2, bias1, bias2, inner, outer, sizes, gain1, shift1, gain2, shift2, flat, wide, t3):
    t = lax.axis_index("tp")
    spread(o, flat)
    to_stored(flat, o_stored)
    spread(dx, wide)
    to_stored(wide, dx_stored)
    d1[...] = grads[0]
    d2[...] = grads[1]
    for start, dst in ((0, tok1), (384, tok2)):
        for j in range(3):
            lanes = slice(start + 128 * j, start + 128 * j + 128)
            t3[j, pl.ds(0, HALF, stride=2), :] = total[0:HALF, lanes]
            t3[j, pl.ds(1, HALF, stride=2), :] = total[GAP : GAP + HALF, lanes]
        for j in range(3):
            dst[:, 128 * j : 128 * j + 128] = t3[j]
    bias1[...] = total[HALF : HALF + 1, 0:384].reshape(384)
    for k in range(4):
        inner[pl.ds(768 * k, 768)] = total[HALF + 1 + k : HALF + 2 + k, :].reshape(768)
    column = jnp.broadcast_to(total[204:205, 0:ROWS], (128, ROWS)).T
    t3[0, pl.ds(0, HALF, stride=2), :] = column[0:HALF]
    t3[0, pl.ds(1, HALF, stride=2), :] = column[GAP : GAP + HALF]
    bias2[...] = t3[0].T[0:1].reshape(S)
    outer[...] = total[205:206, :].reshape(768)
    gg, gb = total[208:272, :], total[272:336, :]
    size = jnp.sqrt(jnp.sum(gg * gg + gb * gb, -1, keepdims=True))
    factor = bound / jnp.maximum(size, bound)
    sizes[...] = jnp.broadcast_to(size, (GROUPS, 128)).T[0:1].reshape(GROUPS)

    def own(v, dst):
        picked = jnp.zeros((1, 192), F32)
        for q in range(4):
            picked = jnp.where(t == q, v[:, 192 * q : 192 * q + 192], picked)
        dst[...] = picked.reshape(192)

    own(total[202:203, :], gain1)
    own(total[203:204, :], shift1)
    own(jnp.sum(factor * gg, 0, keepdims=True), gain2)
    own(jnp.sum(factor * gb, 0, keepdims=True), shift2)


def finish(bound, *operands):
    vmem = pl.BlockSpec(memory_space=pltpu.VMEM)
    shapes = [(16, HALF * 384)] * 2 + [(96, 768)] * 2 + [(S, 384)] * 2 + [(384,), (S,), (3072,), (768,), (GROUPS,)] + [(192,)] * 4
    return pl.pallas_call(functools.partial(finish_kernel, bound),
        out_shape=[jax.ShapeDtypeStruct(v, BF16 if n < 2 else F32) for n, v in enumerate(shapes)],
        in_specs=[vmem] * 4, out_specs=[vmem] * len(shapes),
        scratch_shapes=[pltpu.VMEM((3, 4 * BLOCK, 128), F32), pltpu.VMEM((3, 4 * BLOCK, 128), F32), pltpu.VMEM((3, S, 128), F32)],
        compiler_params=pltpu.CompilerParams(vmem_limit_bytes=32 << 20))(*operands)


epsilon = 1e-06
highest = lax.Precision.HIGHEST


def normalised(values):
    average = jnp.mean(values, -1, keepdims=True)
    inverse = lax.rsqrt(jnp.mean(values * values, -1, keepdims=True) - average * average + epsilon)
    return (values - average) * inverse, inverse


def norm_back(grad_hat, normed, inverse):
    return inverse * (
        grad_hat - jnp.mean(grad_hat, -1, keepdims=True) - normed * jnp.mean(grad_hat * normed, -1, keepdims=True)
    )


def general(block_in, ln1_gain, ln1_shift, tok_w1, tok_b1, tok_w2, tok_b2, ln2_gain, ln2_shift,
               ch_w1, ch_b1, ch_w2, ch_b2, group_ids, out_grad):
    f32 = jnp.float32
    bf16 = jnp.bfloat16
    tp = lax.axis_size("tp")
    dp = lax.axis_size("dp")
    held = block_in.shape[0]
    images = held // tp
    width = block_in.shape[2] // S
    full = width * tp
    t = lax.axis_index("tp")

    def whole_images(stored):
        got = lax.all_to_all(stored.reshape(tp, images, S * width), "tp", 0, 0, tiled=True)
        return got.reshape(tp, images, S, width).transpose(1, 2, 0, 3).reshape(images, S, full)

    def stored(values):
        parts = values.reshape(images, S, tp, width).transpose(2, 0, 1, 3).reshape(tp, images, S * width)
        return lax.all_to_all(parts, "tp", 0, 0, tiled=True).reshape(held, 1, S * width)

    rows = ch_w1.shape[0]
    shard = jnp.stack([ch_w1.astype(bf16), ch_w2.T.astype(bf16)])
    gathered = lax.all_gather(lax.all_gather(shard, "tp", axis=1), "dp", axis=2)
    gathered = gathered.reshape(2, tp, dp * rows, shard.shape[2])
    norms = lax.all_gather(jnp.stack([ln1_gain, ln1_shift, ln2_gain, ln2_shift]), "tp", axis=1, tiled=True)
    x = whole_images(block_in).astype(f32)
    dz_low = whole_images(out_grad)
    token_w1 = tok_w1.astype(bf16)
    token_w2 = tok_w2.astype(bf16)
    xhat, inv_x = normalised(x)
    mixed = (xhat * norms[0] + norms[1]).astype(bf16)
    pre = jnp.einsum("nsc,sk->nkc", mixed, token_w1, preferred_element_type=f32) + tok_b1[:, None]
    hidden, hidden_back = jax.vjp(jax.nn.gelu, pre)
    hidden = hidden.astype(bf16)
    u = x + jnp.einsum("nkc,ks->nsc", hidden, token_w2, preferred_element_type=f32) + tok_b2[:, None]
    uhat, inv_u = normalised(u)
    count = images * S
    hn = (uhat * norms[2] + norms[3]).astype(bf16).reshape(count, full)
    dz = dz_low.reshape(count, full)
    z = jnp.zeros((count, full), f32)
    dhn = jnp.zeros((count, full), f32)
    grads1, grads2, bias = [], [], []
    inner = shard.shape[2]
    for j in range(tp):
        q = jnp.dot(hn, gathered[0, j], preferred_element_type=f32) + ch_b1[j * inner : (j + 1) * inner]
        g, g_back = jax.vjp(jax.nn.gelu, q)
        g = g.astype(bf16)
        z = z + jnp.einsum("rh,ch->rc", g, gathered[1, j], preferred_element_type=f32)
        dg = jnp.dot(dz, gathered[1, j], preferred_element_type=f32)
        dq = g_back(dg)[0].astype(bf16)
        grads2.append(jnp.einsum("rc,rh->ch", dz, g, preferred_element_type=f32).astype(bf16))
        grads1.append(jnp.einsum("rc,rh->ch", hn, dq, preferred_element_type=f32).astype(bf16))
        bias.append(jnp.sum(dq.astype(f32), 0))
        dhn = dhn + jnp.einsum("rh,ch->rc", dq, gathered[0, j], preferred_element_type=f32)
    z = (z + ch_b2).astype(bf16).astype(f32).reshape(u.shape)
    block_out = stored((u + z).astype(bf16))
    dhn = dhn.reshape(u.shape)
    dz32 = dz_low.astype(f32)
    image_gain = jnp.sum(dhn * uhat, 1)
    image_shift = jnp.sum(dhn, 1)
    du = dz32 + norm_back(dhn * norms[2], uhat, inv_u)
    dp_low = du.astype(bf16)
    dh = jnp.einsum("nsc,ks->nkc", dp_low, token_w2, preferred_element_type=f32)
    d_tok_w2 = jnp.einsum("nkc,nsc->ks", hidden, dp_low, preferred_element_type=f32)
    d_tok_b2 = jnp.sum(dp_low.astype(f32), (0, 2))
    dpre = hidden_back(dh)[0].astype(bf16)
    d_tok_w1 = jnp.einsum("nsc,nkc->sk", mixed, dpre, preferred_element_type=f32)
    d_tok_b1 = jnp.sum(dpre.astype(f32), (0, 2))
    da = jnp.einsum("nkc,sk->nsc", dpre, token_w1, preferred_element_type=f32)
    d_gain1 = jnp.sum(da * xhat, (0, 1))
    d_shift1 = jnp.sum(da, (0, 1))
    dx = stored((du + norm_back(da * norms[0], xhat, inv_x)).astype(bf16))

    gradient = jnp.stack([jnp.stack(grads1), jnp.stack(grads2)]).reshape(2, tp, dp, rows, inner)
    owned = lax.psum_scatter(lax.psum_scatter(gradient, "tp", scatter_dimension=1, tiled=True).astype(bf16), "dp", scatter_dimension=2, tiled=True)
    owned = owned.astype(f32).reshape(2, rows, inner)

    ids = lax.dynamic_slice_in_dim(group_ids, t * images, images)
    member = (ids[:, None] == jnp.arange(GROUPS)[None, :]).astype(f32)
    groups = jnp.dot(member.T, jnp.concatenate([image_gain, image_shift], 1), precision=highest)
    flat = [d_tok_w1, d_tok_w2, jnp.stack(bias), jnp.sum(dz32, (0, 1)), d_gain1, d_shift1, d_tok_b1, d_tok_b2, groups]
    sizes = [v.size for v in flat]
    need = sum(sizes)
    unit = 64 * full
    padded = -(-need // unit) * unit
    packed = jnp.concatenate([v.reshape(-1) for v in flat] + [jnp.zeros((padded - need,), f32)]).reshape(-1, full)
    total = lax.psum(packed, ("dp", "tp"))
    total = total.reshape(-1)
    pieces, start = [], 0
    for v in flat:
        pieces.append(total[start : start + v.size].reshape(v.shape))
        start += v.size
    tw1, tw2, cb1, cb2, g1, s1, tb1, tb2, gg = pieces
    gg = gg.reshape(GROUPS, 2, full)
    group_norms = jnp.sqrt(jnp.sum(gg * gg, (1, 2)))
    bound = 2.0 * math.sqrt(held * dp * S * full / GROUPS)
    factor = bound / jnp.maximum(group_norms, bound)
    clipped = jnp.sum(factor[:, None, None] * gg, 0)

    def mine(v):
        return lax.dynamic_slice_in_dim(v, t * width, width)

    return (block_out, dx, group_norms, mine(g1), mine(s1), tw1, tb1, tw2, tb2, mine(clipped[0]), mine(clipped[1]),
            owned[0], cb1.reshape(-1), owned[1].T, cb2)


def blocked(block_in, ln1_gain, ln1_shift, tok_w1, tok_b1, tok_w2, tok_b2, ln2_gain, ln2_shift,
            ch_w1, ch_b1, ch_w2, ch_b2, group_ids, out_grad):
    held = block_in.shape[0]
    bound = 2.0 * math.sqrt(held * 8 * S * 768 / GROUPS)
    flat = (held, HALF * 384)
    w, g, s, u, hn, x, dz, h, ts, op, norms, w1, w2 = forward_pass(
        ch_w1, ch_w2.T, block_in.reshape(flat), out_grad.reshape(flat), ln1_gain, ln1_shift, ln2_gain, ln2_shift,
        tok_w1, tok_w2.T, tok_b1, tok_b2, ch_b1, ch_b2)
    out, dx, grads, total = backward_pass(w, g, s, u, hn, x, dz, h, ts, op, norms, w1, w2, group_ids)
    out, dx, d1, d2, tok1, tok2, bias1, bias2, inner, outer, sizes, gain1, shift1, gain2, shift2 = finish(bound, out, dx, grads, total)
    shape = block_in.shape
    return (out.reshape(shape), dx.reshape(shape), sizes, gain1, shift1, tok1, bias1, tok2.T, bias2,
            gain2, shift2, d1, inner, d2.T, outer)


def solution(mesh):
    stored, own, copied = P("dp", "tp", None), P("tp"), P()
    in_specs = (stored, own, own, copied, copied, copied, copied, own, own, P("dp", "tp"), copied, P("tp", "dp"), copied, P("dp"), stored)
    out_specs = (stored, stored, copied, own, own, copied, copied, copied, copied, own, own, P("dp", "tp"), copied, P("tp", "dp"), copied)
    step = blocked if (mesh.shape["dp"], mesh.shape["tp"]) == (8, 4) else general
    return jax.shard_map(step, mesh=mesh, in_specs=in_specs, out_specs=out_specs, check_vma=False)
```

time: 241 us -> 179 us (0.74)
  Pallas kernels: 206 us -> 173 us
  local copies, waits for them, and re-layouts: 26.5 us -> 4.88 us
  other arithmetic: 7.55 us -> 0 us
    pallas_call x1 -> x2, Pallas kernels: 117 us -> 94.8 us  [the longest x1 92.3 us: backward_pass(): pl.pallas_call(backward_kernel, out_shape=[sds(packed, BF16), sds(packed,...]
    reshape x11 -> x0, local copies, waits for them, and re-layouts: 14 us -> none  [the longest x1 2.69 us: blocked(): out_grad.reshape(4, 4 * HALF, 384)]
    pallas_call x1, Pallas kernels: 89.3 us -> 78 us  [forward_pass(): pl.pallas_call(forward_kernel, out_shape=[sds(*v) for v in shapes], in_sp...]
    another operation x10 -> x0, other arithmetic: 4.61 us -> none
    slice x7 -> x0, local copies, waits for them, and re-layouts: 4.58 us -> none  [the longest x1 1.34 us: blocked(): total[205]]
    unnamed x30 -> x8, local copies, waits for them, and re-layouts: 0.42 us -> 4.88 us
    another operation x7 -> x0, local copies, waits for them, and re-layouts: 2.77 us -> none  [the longest x5 2.46 us: whole(): jnp.stack(parts, axis + 1)]
    transpose x3 -> x0, local copies, waits for them, and re-layouts: 2.47 us -> none  [the longest x2 1.62 us: blocked(): w, g, s, u, hn, x, dz, h, ts, op, norms = forward_pass(shard, xs, ds, lnp...]
where the time goes in v1:
time: 179 us
  Pallas kernels  173 us (97%)
  local copies, waits for them, and re-layouts  4.88 us (3%)
    pallas_call x1, Pallas kernels, backward_pass(): pl.pallas_call(backward_kernel, out_shape=[sds(packed, BF16), sds(packed,...  92.3 us
    pallas_call x1, Pallas kernels, forward_pass(): pl.pallas_call(forward_kernel, out_shape=[sds(*v) for v in shapes], in_sp...  78 us
    unnamed x8, local copies, waits for them, and re-layouts  4.88 us

profile of v1, /device:TPU:0, one launch (start us, length us, event | category | flops | bytes accessed | tf_op | source)
XLA Modules:
  0.0 178.6 jit_solution(4421584039579935811)
XLA Ops:
  0.7 78.0 %shard_map.262 = (bf16[2,4,8,96,768]{4,3,2,1,0:T(8,128)(2,1)}, bf16[4,4,208,768]{3,2,1,0:T(8,128)(2,1)}, bf16[4,4,208,768]{3,2,1,0:T(8,128)(2,1)}, f32[4,208,768...) custom-call(f32[96,768]{1,0:T(8,128)} %cw1.1, ...), custom_call_target="tpu_custom_call" | custom-call | tf_op jit(solution)/shard_map/pallas_call | solution.py:360
  78.7 92.3 %shard_map.263 = (bf16[4,392,384]{2,1,0:T(8,128)(2,1)}, bf16[4,392,384]{2,1,0:T(8,128)(2,1)}, f32[2,96,768]{2,1,0:T(8,128)}, f32[384,768]{1,0:T(8,128)}) custom-call(bf16[2,4,8,96,768]{4,3,2,1,0:T(8,128)(2,1)} %get-tuple-element.47.w_in, bf16[4,4,208,768]{3,2,1,0:T(8,128)(2,1)} %get-tuple-element.48.g_in, bf16[4,4,208,768]{3,2,1,0:T(8,128)(2,1)} %get-tuple-element.49.s_in, ...), custom_call_target="tpu_custom_call" | custom-call | tf_op jit(solution)/shard_map/pallas_call | solution.py:639
  171.0 0.0 copy-start
  171.0 1.3 copy-done
  172.2 0.0 copy-start.1
  172.3 1.3 copy-done.1
  173.5 0.0 copy-start.2
  173.5 1.3 copy-done.2
  174.8 0.0 copy-start.3
  174.8 1.1 copy-done.3
  175.9 2.6 %shard_map.264 = (bf16[16,37632]{1,0:T(8,128)(2,1)}, bf16[16,37632]{1,0:T(8,128)(2,1)}, f32[96,768]{1,0:T(8,128)}, f32[96,768]{1,0:T(8,128)}, f32[196,384]{1,0:T...) custom-call(bf16[4,392,384]{2,1,0:T(8,128)(2,1)S(1)} %copy-done, ...), custom_call_target="tpu_custom_call" | custom-call | tf_op jit(solution)/shard_map/pallas_call | solution.py:695
Async XLA Ops:
  171.0 1.3 copy-start
  172.2 1.3 copy-start.1
  173.5 1.3 copy-start.2
  174.8 1.1 copy-start.3

commit v2 on v1

v2 whole, which is shorter than its diff:
```python
import functools
import math

import jax
import jax.numpy as jnp
from jax import lax
from jax.experimental import pallas as pl
from jax.experimental.pallas import tpu as pltpu
from jax.sharding import PartitionSpec as P

MESH = pl.DeviceIdType.MESH


S = 196
GROUPS = 64
F32 = jnp.float32
BF16 = jnp.bfloat16
HALF = 98
GAP = 104
ROWS = 208
BLOCK = 4 * HALF
LOW = math.sqrt(2.0 / math.pi)
CUBE = 0.044715


def place():
    dp = lax.axis_index("dp")
    t = lax.axis_index("tp")
    c, x, y = dp % 2, (dp // 2) % 2, dp // 4
    near = dict(S=owner(y, x, 1 - c), X=owner(y, 1 - x, c), Y=owner(1 - y, x, c), D=owner(1 - y, 1 - x, c))
    return dp, t, near, (y, x, c)


def owner(y, x, c):
    return (y * 2 + x) * 2 + c


def others(t):
    first = jnp.where(t == 0, 1, jnp.where(t == 1, 0, jnp.where(t == 2, 3, 2)))
    second = jnp.where(t == 0, 2, jnp.where(t == 1, 2, 1))
    third = jnp.where(t < 2, 3, 0)
    return [first, second, third]


def meet(devices):
    barrier = pltpu.get_barrier_semaphore()
    for device in devices:
        pl.semaphore_signal(barrier, inc=1, device_id=device, device_id_type=MESH)
    pl.semaphore_wait(barrier, len(devices))


def remote(src, dst, ss, rs, device):
    return pltpu.make_async_remote_copy(src_ref=src, dst_ref=dst, send_sem=ss, recv_sem=rs, device_id=device, device_id_type=MESH)


def gelu_pair(v):
    square = v * v
    up = 0.5 * jnp.tanh(v * (LOW + (LOW * CUBE) * square)) + 0.5
    value = v * up
    slope = up + value * (1.0 - up) * (2.0 * LOW + (6.0 * LOW * CUBE) * square)
    return value, slope


def turn(v):
    return pltpu.roll(v, 64, 1)


def lane_low():
    return lax.broadcasted_iota(jnp.int32, (HALF, 128), 1) < 64


def join_groups(flat, image, store):
    low = lane_low()
    for p in range(2):
        a = [flat[j, pl.ds(2 * p * BLOCK + image * HALF, HALF), :] for j in range(3)]
        b = [flat[j, pl.ds((2 * p + 1) * BLOCK + image * HALF, HALF), :] for j in range(3)]
        a1, a2, b0, b1 = turn(a[1]), turn(a[2]), turn(b[0]), turn(b[1])
        even = [a[0], jnp.where(low, a[1], b0), jnp.where(low, b0, b1)]
        odd = [jnp.where(low, a1, a2), jnp.where(low, a2, b[1]), b[2]]
        for j in range(3):
            store(0, 384 * p + 128 * j, even[j])
            store(GAP, 384 * p + 128 * j, odd[j])


def split_groups(load, flat, image):
    low = lane_low()
    for p in range(2):
        e = [load(0, 384 * p + 128 * j) for j in range(3)]
        o = [load(GAP, 384 * p + 128 * j) for j in range(3)]
        e1, e2, o0, o1 = turn(e[1]), turn(e[2]), turn(o[0]), turn(o[1])
        a = [e[0], jnp.where(low, e[1], o0), jnp.where(low, o0, o1)]
        b = [jnp.where(low, e1, e2), jnp.where(low, e2, o[1]), o[2]]
        for j in range(3):
            flat[j, pl.ds(2 * p * BLOCK + image * HALF, HALF), :] = a[j]
            flat[j, pl.ds((2 * p + 1) * BLOCK + image * HALF, HALF), :] = b[j]


def spread(packed, flat):
    for k in range(4):
        for j in range(3):
            flat[j, pl.ds(k * BLOCK, BLOCK), :] = packed[k, :, 128 * j : 128 * j + 128].astype(F32)


def pack(flat, packed):
    for k in range(4):
        for j in range(3):
            packed[k, :, 128 * j : 128 * j + 128] = flat[j, pl.ds(k * BLOCK, BLOCK), :].astype(BF16)


def to_rows(stored, flat):
    for i in range(HALF):
        for j in range(3):
            start = 384 * i + 128 * j
            flat[j, pl.ds(i, 16, stride=HALF), :] = stored[:, start : start + 128].astype(F32)


def to_stored(flat, stored):
    for i in range(HALF):
        for j in range(3):
            start = 384 * i + 128 * j
            stored[:, start : start + 128] = flat[j, pl.ds(i, 16, stride=HALF), :].astype(BF16)


def hat(v):
    average = jnp.mean(v, -1, keepdims=True)
    inverse = lax.rsqrt(jnp.mean(v * v, -1, keepdims=True) - average * average + 1e-06)
    return (v - average) * inverse, inverse


def dot(a, b):
    return jnp.dot(a, b, preferred_element_type=F32)


def dot_nt(a, b):
    return lax.dot_general(a, b, (((1,), (1,)), ((), ())), preferred_element_type=F32)


PIECE = 48
SMALL = 8 * PIECE
DIRECT = (0, 1)


def step_kernel(cw1, cw2, xin, din, p0, p1, p2, p3, tw1, tw2, b1, b2, cb1, cb2, ids,
                o_out, dx_out, w_grad, total_out,
                wf, shard, wv, stored, xs, ds, xr, dr, flat, xb, u, act, hnt, dzt, g, s, h, ts, zs, lr, lall, t3, c2, w1, w2, w1t, w2t,
                sib, first, second, final, zz, small, low, t_sib, t_chip, t_line,
                send_sem, recv_sem, line_sem, x_send, x_recv, d_send, d_recv, ln_send, ln_recv, in_sem, own_sem,
                o_send, o_recv, y_send, y_recv, sib_sem, sib_recv, a_send, a_recv, z_send, z_recv,
                p_send, p_recv, c_send, c_recv, l_send, l_recv, b_send, b_recv, e_send, e_recv):
    dp, t, near, (y, xx, c) = place()
    line = others(t)
    order = [t] + line
    back = [line[2], line[1], line[0], t]
    chips = {"O": (y, xx), "X": (y, 1 - xx), "Y": (1 - y, xx), "D": (1 - y, 1 - xx)}
    slot = {"O": 0, "X": 1, "Y": 2, "D": 3}
    started = {"w": [], "x": [], "y": [], "": []}
    maybe = []
    state = {}
    zero = jnp.zeros((1, 768), F32)

    def go(copy, kind=""):
        copy.start()
        started[kind].append(copy)

    def local(src, dst, sem):
        copy = pltpu.make_async_copy(src, dst, sem)
        copy.start()
        return copy

    def sent(kind):
        for copy in started[kind]:
            copy.wait_send()
        started[kind] = []

    in_w1, in_w2 = local(cw1, wf.at[0], in_sem.at[0]), local(cw2, wf.at[1], in_sem.at[1])
    state["in"] = local(xin, stored, in_sem.at[2])
    meet([(near["S"], t), (near["X"], t), (near["Y"], t), (near["D"], t)] + [(dp, p) for p in line])
    sends = [0, 0]


    def send(src, who, tt, device):
        go(remote(src, wv.at[:, tt, who], send_sem.at[sends[0]], recv_sem.at[who, tt], device), "w")
        sends[0] += 1

    def along(src, tt, target):
        inside = (target >= 0) & (target <= 3)
        copy = remote(src, wv.at[:, tt, dp], line_sem.at[sends[1]], recv_sem.at[dp, tt], (dp, jnp.clip(target, 0, 3)))
        sends[1] += 1
        pl.when(inside)(copy.start)
        maybe.append((inside, copy))

    def arrived(who, tt):
        ref = wv.at[:, tt, who]
        remote(ref, ref, send_sem.at[0], recv_sem.at[who, tt], (dp, t)).wait_recv()

    def weights():
        in_w1.wait()
        in_w2.wait()
        shard[...] = wf[...].astype(BF16)
        along(shard, t, t + 1)
        along(shard, t, t - 1)
        for name in "XYS":
            send(shard, dp, t, (near[name], t))
        wv[:, t, dp] = shard[...]
        for n, ref in enumerate((p0, p1, p2, p3)):
            row = ref[...].reshape(1, 192)
            wide = jnp.concatenate([row, row, row, row], 1)
            lane = lax.broadcasted_iota(jnp.int32, (1, 768), 1)
            lr[t, n : n + 1, :] = jnp.where((lane >= 192 * t) & (lane < 192 * t + 192), wide, 0.0)
        for n, p in enumerate(line):
            go(remote(lr.at[t], lr.at[t], ln_send.at[n], ln_recv.at[t], (dp, p)))

    def column(k):
        tt = order[k]
        arrived(dp, tt)
        src = wv.at[:, tt, dp]
        along(src, tt, jnp.where(tt < t, t + 1, t - 1))
        for name in "XYS":
            send(src, dp, tt, (near[name], t))

    def neighbours(k):
        tt = order[k]
        one, two = ("X", "Y") if k % 2 == 0 else ("Y", "X")
        arrived(near[one], tt)
        src = wv.at[:, tt, near[one]]
        send(src, near[one], tt, (near[two], t))
        send(src, near[one], tt, (near["S"], t))
        arrived(near[two], tt)
        send(wv.at[:, tt, near[two]], near[two], tt, (near["S"], t))

    def diagonal(k):
        tt = order[k]
        arrived(near["D"], tt)
        send(wv.at[:, tt, near["D"]], near["D"], tt, (near["S"], t))


    def pack_input():
        state["in"].wait()
        to_rows(stored, flat)
        pack(flat, xs)
        state["in"] = local(din, stored, in_sem.at[3])

    def send_input(n):
        p = line[n]
        go(remote(xs.at[p], xr.at[t], x_send.at[n], x_recv.at[t], (dp, p)), "x")

    def pack_grad():
        state["in"].wait()
        to_rows(stored, flat)
        pack(flat, ds)

    def send_grad(n):
        p = line[n]
        go(remote(ds.at[p], dr.at[t], d_send.at[n], d_recv.at[t], (dp, p)), "y")

    def token_weights():
        gap = jnp.zeros((GAP - HALF, 128), F32)
        for n, (src, dst) in enumerate(((tw1, w1), (tw2, w2t))):
            for j in range(3):
                t3[j] = src[:, 128 * j : 128 * j + 128]
            for j in range(3):
                even, odd = t3[j, pl.ds(0, HALF, stride=2), :], t3[j, pl.ds(1, HALF, stride=2), :]
                dst[:, 128 * j : 128 * j + 128] = jnp.concatenate([even, gap, odd, gap], 0).astype(BF16)
        w1t[...] = w1[...].T
        w2[...] = w2t[...].T
        c2[...] = jnp.broadcast_to(b2[...].reshape(1, S), (128, S)).T
        few = jnp.zeros((GAP - HALF, 1), F32)
        state["shift2"] = jnp.concatenate([c2[pl.ds(0, HALF, stride=2), :][:, 0:1], few, c2[pl.ds(1, HALF, stride=2), :][:, 0:1], few], 0)
        state["shift1"] = jnp.broadcast_to(b1[...].reshape(1, 384), (8, 384)).T[:, 0:1]
        small[...] = jnp.zeros((SMALL, 768), F32)

    def join(received, own, dst):
        received[t] = own[t]
        spread(received, flat)
        few = jnp.zeros((GAP - HALF, 768), F32)
        for n in range(4):
            for start in (HALF, GAP + HALF):
                zs[n, start : start + GAP - HALF, :] = few

            def put(row, lane, v, n=n):
                zs[n, row : row + HALF, lane : lane + 128] = v

            join_groups(flat, n, put)
            dst[n] = zs[n].astype(BF16)

    def join_input():
        for p in line:
            remote(lr.at[p], lr.at[p], ln_send.at[0], ln_recv.at[p], (dp, t)).wait_recv()
        lall[...] = (lr[0] + lr[1]) + (lr[2] + lr[3])
        for p in line:
            remote(xr.at[p], xr.at[p], x_send.at[0], x_recv.at[p], (dp, t)).wait_recv()
        join(xr, xs, xb)

    def token_forward(start, stop):
        g1, s1, g2, s2 = lall[0:1], lall[1:2], lall[2:3], lall[3:4]
        shift1, shift2 = state["shift1"], state["shift2"]

        def body(n, carry):
            v = xb[n].astype(F32)
            xhat, _ = hat(v)
            a = (xhat * g1 + s1).astype(BF16)
            value, slope = gelu_pair(dot(w1t[...], a) + shift1)
            low = value.astype(BF16)
            h[n] = low
            ts[n] = slope.astype(BF16)
            r = v + dot(w2t[...], low) + shift2
            u[n] = r
            uhat, _ = hat(r)
            act[n] = (uhat * g2 + s2).astype(BF16)
            return carry

        lax.fori_loop(start, stop, body, 0)

    def block(k):
        tt = order[k]
        for name in "OXYD":
            arrived(owner(*chips[name], 1 - c), tt)
        bias = cb1[pl.ds(pl.multiple_of(tt * 768, 128), 768)].reshape(1, 768)

        def body(n, carry):
            value, slope = gelu_pair(dot(act[n], wv[0, tt].reshape(768, 768)) + bias)
            low = value.astype(BF16)
            g[tt, n] = low
            s[tt, n] = slope.astype(BF16)
            part = dot_nt(low, wv[1, tt].reshape(768, 768))
            if k == 0:
                zs[n] = part
            elif k < 3:
                zs[n] += part
            else:
                zs[n] = u[n] + (zs[n] + part + cb2[...].reshape(1, 768)).astype(BF16).astype(F32)
            return carry

        lax.fori_loop(0, 4, body, 0)

    def pack_output():
        for n in range(4):
            split_groups(lambda row, lane, n=n: zs[n, row : row + HALF, lane : lane + 128], flat, n)
        sent("x")
        pack(flat, xs)
        state["own_o"] = local(xs.at[t], o_out.at[t], own_sem.at[0])

    def send_output(n):
        p = line[n]
        go(remote(xs.at[p], o_out.at[t], o_send.at[n], o_recv.at[t], (dp, p)))

    def hidden_in():
        for n in range(4):
            hnt[:, n * ROWS : (n + 1) * ROWS] = act[n].T

    def join_grad():
        for p in line:
            remote(dr.at[p], dr.at[p], d_send.at[0], d_recv.at[p], (dp, t)).wait_recv()
        join(dr, ds, act)
        for n in range(4):
            dzt[:, n * ROWS : (n + 1) * ROWS] = act[n].T
        sent("w")
        for inside, copy in maybe:
            pl.when(inside)(copy.wait_send)
        maybe.clear()


    def hand_over(j, k):
        for name in "DXYO":
            n = slot[name]
            go(remote(wv.at[j, back[k], owner(*chips[name], 1 - c)], sib.at[j, k, n], sib_sem.at[j, k, n], sib_recv.at[j, k, n], (near["S"], t)))

    def chip_sum(j, k, name):
        n = slot[name]
        remote(sib.at[j, k, n], sib.at[j, k, n], sib_sem.at[j, k, n], sib_recv.at[j, k, n], (near["S"], t)).wait_recv()
        sib[j, k, n] = wv[j, back[k], owner(*chips[name], c)] + sib[j, k, n]

    def ways(k):
        return ("X", "Y") if k % 2 == 0 else ("Y", "X")

    def hop(j, k, src, dst, n, name):
        go(remote(src, dst, a_send.at[j, k, n], a_recv.at[j, k, n], (near[name], t)))

    def landed(j, k, dst, n):
        remote(dst, dst, a_send.at[j, k, n], a_recv.at[j, k, n], (near["S"], t)).wait_recv()

    def stage_one(j, k):
        f, s2 = ways(k)
        chip_sum(j, k, "D")
        hop(j, k, sib.at[j, k, 3], first.at[j, k], 0, s2)
        chip_sum(j, k, s2)
        hop(j, k, sib.at[j, k, slot[s2]], second.at[j, k], 1, s2)

    def stage_two(j, k):
        f, s2 = ways(k)
        n = slot[f]
        chip_sum(j, k, f)
        landed(j, k, first.at[j, k], 0)
        sib[j, k, n] = sib[j, k, n] + first[j, k]
        hop(j, k, sib.at[j, k, n], final.at[j, k], 2, f)

    def stage_three(j, k):
        chip_sum(j, k, "O")
        landed(j, k, second.at[j, k], 1)
        landed(j, k, final.at[j, k], 2)
        total = sib[j, k, 0].astype(F32) + second[j, k].astype(F32) + final[j, k].astype(F32)
        if k < 3:
            sib[j, k, 0] = total.astype(BF16)
            if j in DIRECT:
                go(remote(sib.at[j, k, 0], zz.at[j, t], z_send.at[j, k], z_recv.at[j, t], (dp, back[k])))
        else:
            w_grad[j] = total

    def along_in(j, n):
        remote(zz.at[j, n], zz.at[j, n], z_send.at[j, 0], z_recv.at[j, n], (dp, t)).wait_recv()

    def stage_four(j, k):
        p = back[k]
        piece = sib.at[j, k, 0]
        up = remote(piece, zz.at[j, p], z_send.at[j, k], z_recv.at[j, p], (dp, jnp.clip(t + 1, 0, 3)))
        n = jnp.where(t - 1 == p, 4, p)
        down = remote(piece, zz.at[j, n], z_send.at[j, k], z_recv.at[j, n], (dp, jnp.clip(t - 1, 0, 3)))

        @pl.when(((p > t) & (t > 0)) | ((p < t) & (t < 3)))
        def _():
            along_in(j, p)
            piece[...] = piece[...] + zz[j, p]

        pl.when(p > t)(up.start)
        pl.when(p < t)(down.start)
        maybe.append((p > t, up))
        maybe.append((p < t, down))

    def stage_five(j):
        if j in DIRECT:
            for p in line:
                along_in(j, p)
                w_grad[j] += zz[j, p].astype(F32)
            return

        @pl.when(t > 0)
        def _():
            along_in(j, t)
            w_grad[j] += zz[j, t].astype(F32)

        @pl.when(t < 3)
        def _():
            along_in(j, 4)
            w_grad[j] += zz[j, 4].astype(F32)

    def second_weight(k):
        wv[1, back[k]] = dot(dzt[...], g[back[k]].reshape(4 * ROWS, 768)).astype(BF16).reshape(8, 96, 768)
        hand_over(1, k)

    def data(k):
        tt = back[k]

        def body(n, bias):
            low = (dot(act[n], wv[1, tt].reshape(768, 768)) * s[tt, n].astype(F32)).astype(BF16)
            s[tt, n] = low
            part = dot_nt(low, wv[0, tt].reshape(768, 768))
            if k == 0:
                zs[n] = part
            else:
                zs[n] += part
            return bias + jnp.sum(low.astype(F32), 0, keepdims=True)

        small[pl.ds(HALF + 1 + tt, 1), :] = lax.fori_loop(0, 4, body, zero)

    def first_weight(k):
        wv[0, back[k]] = dot(hnt[...], s[back[k]].reshape(4 * ROWS, 768)).astype(BF16).reshape(8, 96, 768)
        hand_over(0, k)

    def token_backward(start, stop):
        g1, s1, g2 = lall[0:1], lall[1:2], lall[2:3]
        row = lax.broadcasted_iota(jnp.int32, (ROWS, 768), 0)
        ones = jnp.ones((8, 768), BF16)
        groups = lax.broadcasted_iota(jnp.int32, (GROUPS, 16), 0) == ids[...].reshape(1, 16)
        lane = lax.broadcasted_iota(jnp.int32, (GROUPS, 16), 1)

        def body(n, carry):
            sum_g1, sum_s1, sum_b2, sum_dz = carry
            d, grad = zs[n], act[n].astype(F32)
            uhat, inv_u = hat(u[n])
            member = jnp.sum(jnp.where(groups & (lane == 4 * t + n), 1.0, 0.0), -1, keepdims=True)
            small[208:272, :] += member * jnp.sum(d * uhat, 0, keepdims=True)
            small[272:336, :] += member * jnp.sum(d, 0, keepdims=True)
            e = d * g2
            du = grad + inv_u * (e - jnp.mean(e, -1, keepdims=True) - uhat * jnp.mean(e * uhat, -1, keepdims=True))
            low = du.astype(BF16)
            dpre = (dot(w2[...], low) * ts[n].astype(F32)).astype(BF16)
            xhat, inv_x = hat(xb[n].astype(F32))
            a = jnp.where(row == HALF, 1.0, xhat * g1 + s1).astype(BF16)
            tok1 = dot_nt(a, dpre)
            tok2 = dot_nt(low, h[n])
            for begin, size in ((0, HALF + 1), (GAP, HALF)):
                small[begin : begin + size, 0:384] += tok1[begin : begin + size]
            for begin, size in ((0, HALF), (GAP, HALF)):
                small[begin : begin + size, 384:768] += tok2[begin : begin + size]
            da = dot(w1[...], dpre)
            e1 = da * g1
            zs[n] = du + inv_x * (e1 - jnp.mean(e1, -1, keepdims=True) - xhat * jnp.mean(e1 * xhat, -1, keepdims=True))
            return (sum_g1 + jnp.sum(da * xhat, 0, keepdims=True), sum_s1 + jnp.sum(da, 0, keepdims=True),
                    sum_b2 + dot_nt(ones, low), sum_dz + jnp.sum(grad, 0, keepdims=True))

        sums = state.get("sums", (zero, zero, jnp.zeros((8, ROWS), F32), zero))
        state["sums"] = lax.fori_loop(start, stop, body, sums)

    def pack_dx():
        for n in range(4):
            split_groups(lambda r, lane, n=n: zs[n, r : r + HALF, lane : lane + 128], flat, n)
        sent("y")
        pack(flat, ds)
        state["own_x"] = local(ds.at[t], dx_out.at[t], own_sem.at[1])

    def send_dx(n):
        p = line[n]
        go(remote(ds.at[p], dx_out.at[t], y_send.at[n], y_recv.at[t], (dp, p)))

    chip = dp // 2
    far = [("X", near["X"] // 2), ("Y", near["Y"] // 2), ("D", near["D"] // 2)]

    def part(ref, core, q):
        return ref.at[pl.ds(pl.multiple_of((core * 4 + q) * PIECE, 8), PIECE)]

    def half(ref, core):
        return ref.at[pl.ds(pl.multiple_of(core * 4 * PIECE, 8), 4 * PIECE)]

    own = part(total_out, c, chip)

    def total_zero():
        sum_g1, sum_s1, sum_b2, sum_dz = state["sums"]
        small[202:203, :] = sum_g1
        small[203:204, :] = sum_s1
        small[204:205, 0:ROWS] = sum_b2[0:1]
        small[205:206, :] = sum_dz
        half(low, 1 - c)[...] = half(small, 1 - c)[...].astype(BF16)
        go(remote(half(low, 1 - c), t_sib, p_send, p_recv, (near["S"], t)))

    def total_one():
        remote(t_sib, t_sib, p_send, p_recv, (near["S"], t)).wait_recv()
        both = half(small, c)[...] + t_sib[...].astype(F32)
        half(small, c)[...] = both
        half(low, c)[...] = both.astype(BF16)
        for n, (name, q) in enumerate(far):
            go(remote(part(low, c, q), t_chip.at[n], c_send.at[n], c_recv.at[n], (near[name], t)))

    def total_two():
        total = part(small, c, chip)[...]
        for n in range(3):
            remote(t_chip.at[n], t_chip.at[n], c_send.at[n], c_recv.at[n], (near["S"], t)).wait_recv()
            total = total + t_chip[n].astype(F32)
        t_line[t] = total.astype(BF16)
        for n, p in enumerate(line):
            go(remote(t_line.at[t], t_line.at[t], l_send.at[n], l_recv.at[t], (dp, p)))

    def total_three():
        for p in line:
            remote(t_line.at[p], t_line.at[p], l_send.at[0], l_recv.at[p], (dp, t)).wait_recv()
        sums = [t_line[p].astype(F32) for p in range(4)]
        own[...] = (((sums[0] + sums[1]) + sums[2]) + sums[3]).astype(BF16)
        for n, (name, q) in enumerate(far):
            go(remote(own, own, b_send.at[n], b_recv.at[chip], (near[name], t)))
        go(remote(own, own, e_send.at[3], e_recv.at[chip], (near["S"], t)))

    def total_five():
        for n, (name, q) in enumerate(far):
            there = part(total_out, c, q)
            remote(there, there, b_send.at[0], b_recv.at[q], (dp, t)).wait_recv()
            go(remote(there, there, e_send.at[n], e_recv.at[q], (near["S"], t)))

    def total_six():
        for q in range(4):
            there = part(total_out, 1 - c, q)
            remote(there, there, e_send.at[0], e_recv.at[q], (dp, t)).wait_recv()

    weights()
    pack_input()
    column(1)
    neighbours(0)
    column(2)
    send_input(0)
    send_input(1)
    send_input(2)
    neighbours(1)
    diagonal(0)
    column(3)
    pack_grad()
    token_weights()
    neighbours(2)
    diagonal(1)
    neighbours(3)
    diagonal(2)
    diagonal(3)
    join_input()
    send_grad(0)
    send_grad(1)
    send_grad(2)
    token_forward(0, 4)
    block(0)
    block(1)
    block(2)
    block(3)
    pack_output()
    send_output(0)
    send_output(1)
    send_output(2)
    hidden_in()
    join_grad()
    data(0)
    second_weight(0)
    data(1)
    second_weight(1)
    stage_one(1, 0)
    data(2)
    second_weight(2)
    stage_one(1, 1)
    data(3)
    second_weight(3)
    stage_one(1, 2)
    stage_one(1, 3)
    stage_two(1, 0)
    token_backward(0, 2)
    stage_two(1, 1)
    stage_two(1, 2)
    token_backward(2, 4)
    pack_dx()
    send_dx(0)
    send_dx(1)
    send_dx(2)
    total_zero()
    stage_two(1, 3)
    stage_three(1, 0)
    first_weight(0)
    total_one()
    first_weight(1)
    stage_three(1, 1)
    stage_one(0, 0)
    first_weight(2)
    stage_one(0, 1)
    first_weight(3)
    stage_one(0, 2)
    stage_three(1, 2)
    stage_one(0, 3)
    total_two()
    stage_three(1, 3)
    stage_two(0, 0)
    stage_two(0, 1)
    total_three()
    stage_two(0, 2)
    stage_two(0, 3)
    stage_three(0, 0)
    stage_three(0, 1)
    stage_three(0, 2)
    stage_three(0, 3)
    total_five()
    stage_five(1)
    stage_five(0)
    total_six()

    state["own_o"].wait()
    state["own_x"].wait()
    for p in line:
        remote(o_out.at[p], o_out.at[p], o_send.at[0], o_recv.at[p], (dp, t)).wait_recv()
        remote(dx_out.at[p], dx_out.at[p], y_send.at[0], y_recv.at[p], (dp, t)).wait_recv()
    sent("")
    for inside, copy in maybe:
        pl.when(inside)(copy.wait_send)


def one_step(*operands):
    any_, vmem = pl.BlockSpec(memory_space=pl.ANY), pl.BlockSpec(memory_space=pltpu.VMEM)
    sds = jax.ShapeDtypeStruct
    dma = pltpu.SemaphoreType.DMA
    V = pltpu.VMEM
    wshape, act, tok, packed, piece = (2, 4, 8, 96, 768), (4, ROWS, 768), (4, 384, 768), (4, BLOCK, 384), (96, 768)
    return pl.pallas_call(step_kernel,
        out_shape=[sds(packed, BF16), sds(packed, BF16), sds((2,) + piece, F32), sds((SMALL, 768), BF16)],
        in_specs=[any_] * 4 + [vmem] * 11, out_specs=[any_] * 2 + [vmem] * 2,
        scratch_shapes=[V((2, 96, 768), F32), V((2, 96, 768), BF16), V(wshape, BF16), V((16, HALF * 384), BF16), V(packed, BF16), V(packed, BF16),
            V(packed, BF16), V(packed, BF16), V((3, 4 * BLOCK, 128), F32), V(act, BF16), V(act, F32), V(act, BF16), V((768, 4 * ROWS), BF16), V((768, 4 * ROWS), BF16),
            V((4,) + act, BF16), V((4,) + act, BF16), V(tok, BF16), V(tok, BF16), V(act, F32), V((4, 8, 768), F32), V((8, 768), F32),
            V((3, S, 128), F32), V((S, 128), F32), V((ROWS, 384), BF16), V((384, ROWS), BF16), V((384, ROWS), BF16), V((ROWS, 384), BF16),
            V((2, 4, 4) + piece, BF16), V((2, 4) + piece, BF16), V((2, 4) + piece, BF16), V((2, 4) + piece, BF16), V((2, 5) + piece, BF16),
            V((SMALL, 768), F32), V((SMALL, 768), BF16), V((4 * PIECE, 768), BF16), V((3, PIECE, 768), BF16), V((4, PIECE, 768), BF16),
            dma((28,)), dma((8, 4)), dma((5,)), dma((3,)), dma((4,)), dma((3,)), dma((4,)), dma((3,)), dma((4,)), dma((4,)), dma((2,)),
            dma((3,)), dma((4,)), dma((3,)), dma((4,)), dma((2, 4, 4)), dma((2, 4, 4)), dma((2, 4, 3)), dma((2, 4, 3)), dma((2, 4)), dma((2, 5)),
            dma, dma, dma((3,)), dma((3,)), dma((3,)), dma((4,)), dma((3,)), dma((4,)), dma((4,)), dma((4,))],
        compiler_params=pltpu.CompilerParams(collective_id=1, has_side_effects=True, vmem_limit_bytes=63 << 20))(*operands)


def finish_kernel(bound, o_in, dx_in, grads_in, total_in, o_stored, dx_stored, d1, d2, tok1, tok2, bias1, bias2, inner, outer, sizes, gain1, shift1, gain2, shift2, o, dx, grads, low, flat, wide, t3, total, sems):
    t = lax.axis_index("tp")
    copies = [pltpu.make_async_copy(src, dst, sems.at[n]) for n, (src, dst) in enumerate(((total_in, low), (o_in, o), (dx_in, dx), (grads_in, grads)))]
    for copy in copies:
        copy.start()
    for copy in copies:
        copy.wait()
    total[...] = low[...].astype(F32)
    spread(o, flat)
    to_stored(flat, o_stored)
    spread(dx, wide)
    to_stored(wide, dx_stored)
    d1[...] = grads[0]
    d2[...] = grads[1]
    for start, dst in ((0, tok1), (384, tok2)):
        for j in range(3):
            lanes = slice(start + 128 * j, start + 128 * j + 128)
            t3[j, pl.ds(0, HALF, stride=2), :] = total[0:HALF, lanes]
            t3[j, pl.ds(1, HALF, stride=2), :] = total[GAP : GAP + HALF, lanes]
        for j in range(3):
            dst[:, 128 * j : 128 * j + 128] = t3[j]
    bias1[...] = total[HALF : HALF + 1, 0:384].reshape(384)
    for k in range(4):
        inner[pl.ds(768 * k, 768)] = total[HALF + 1 + k : HALF + 2 + k, :].reshape(768)
    column = jnp.broadcast_to(total[204:205, 0:ROWS], (128, ROWS)).T
    t3[0, pl.ds(0, HALF, stride=2), :] = column[0:HALF]
    t3[0, pl.ds(1, HALF, stride=2), :] = column[GAP : GAP + HALF]
    bias2[...] = t3[0].T[0:1].reshape(S)
    outer[...] = total[205:206, :].reshape(768)
    gg, gb = total[208:272, :], total[272:336, :]
    size = jnp.sqrt(jnp.sum(gg * gg + gb * gb, -1, keepdims=True))
    factor = bound / jnp.maximum(size, bound)
    sizes[...] = jnp.broadcast_to(size, (GROUPS, 128)).T[0:1].reshape(GROUPS)

    def own(v, dst):
        picked = jnp.zeros((1, 192), F32)
        for q in range(4):
            picked = jnp.where(t == q, v[:, 192 * q : 192 * q + 192], picked)
        dst[...] = picked.reshape(192)

    own(total[202:203, :], gain1)
    own(total[203:204, :], shift1)
    own(jnp.sum(factor * gg, 0, keepdims=True), gain2)
    own(jnp.sum(factor * gb, 0, keepdims=True), shift2)


def finish(bound, *operands):
    vmem = pl.BlockSpec(memory_space=pltpu.VMEM)
    shapes = [(16, HALF * 384)] * 2 + [(96, 768)] * 2 + [(S, 384)] * 2 + [(384,), (S,), (3072,), (768,), (GROUPS,)] + [(192,)] * 4
    return pl.pallas_call(functools.partial(finish_kernel, bound),
        out_shape=[jax.ShapeDtypeStruct(v, BF16 if n < 2 else F32) for n, v in enumerate(shapes)],
        in_specs=[pl.BlockSpec(memory_space=pl.ANY)] * 4, out_specs=[vmem] * len(shapes),
        scratch_shapes=[pltpu.VMEM((4, BLOCK, 384), BF16), pltpu.VMEM((4, BLOCK, 384), BF16), pltpu.VMEM((2, 96, 768), F32), pltpu.VMEM((SMALL, 768), BF16),
            pltpu.VMEM((3, 4 * BLOCK, 128), F32), pltpu.VMEM((3, 4 * BLOCK, 128), F32), pltpu.VMEM((3, S, 128), F32), pltpu.VMEM((SMALL, 768), F32), pltpu.SemaphoreType.DMA((4,))],
        compiler_params=pltpu.CompilerParams(vmem_limit_bytes=32 << 20))(*operands)


epsilon = 1e-06
highest = lax.Precision.HIGHEST


def normalised(values):
    average = jnp.mean(values, -1, keepdims=True)
    inverse = lax.rsqrt(jnp.mean(values * values, -1, keepdims=True) - average * average + epsilon)
    return (values - average) * inverse, inverse


def norm_back(grad_hat, normed, inverse):
    return inverse * (
        grad_hat - jnp.mean(grad_hat, -1, keepdims=True) - normed * jnp.mean(grad_hat * normed, -1, keepdims=True)
    )


def general(block_in, ln1_gain, ln1_shift, tok_w1, tok_b1, tok_w2, tok_b2, ln2_gain, ln2_shift,
               ch_w1, ch_b1, ch_w2, ch_b2, group_ids, out_grad):
    f32 = jnp.float32
    bf16 = jnp.bfloat16
    tp = lax.axis_size("tp")
    dp = lax.axis_size("dp")
    held = block_in.shape[0]
    images = held // tp
    width = block_in.shape[2] // S
    full = width * tp
    t = lax.axis_index("tp")

    def whole_images(stored):
        got = lax.all_to_all(stored.reshape(tp, images, S * width), "tp", 0, 0, tiled=True)
        return got.reshape(tp, images, S, width).transpose(1, 2, 0, 3).reshape(images, S, full)

    def stored(values):
        parts = values.reshape(images, S, tp, width).transpose(2, 0, 1, 3).reshape(tp, images, S * width)
        return lax.all_to_all(parts, "tp", 0, 0, tiled=True).reshape(held, 1, S * width)

    rows = ch_w1.shape[0]
    shard = jnp.stack([ch_w1.astype(bf16), ch_w2.T.astype(bf16)])
    gathered = lax.all_gather(lax.all_gather(shard, "tp", axis=1), "dp", axis=2)
    gathered = gathered.reshape(2, tp, dp * rows, shard.shape[2])
    norms = lax.all_gather(jnp.stack([ln1_gain, ln1_shift, ln2_gain, ln2_shift]), "tp", axis=1, tiled=True)
    x = whole_images(block_in).astype(f32)
    dz_low = whole_images(out_grad)
    token_w1 = tok_w1.astype(bf16)
    token_w2 = tok_w2.astype(bf16)
    xhat, inv_x = normalised(x)
    mixed = (xhat * norms[0] + norms[1]).astype(bf16)
    pre = jnp.einsum("nsc,sk->nkc", mixed, token_w1, preferred_element_type=f32) + tok_b1[:, None]
    hidden, hidden_back = jax.vjp(jax.nn.gelu, pre)
    hidden = hidden.astype(bf16)
    u = x + jnp.einsum("nkc,ks->nsc", hidden, token_w2, preferred_element_type=f32) + tok_b2[:, None]
    uhat, inv_u = normalised(u)
    count = images * S
    hn = (uhat * norms[2] + norms[3]).astype(bf16).reshape(count, full)
    dz = dz_low.reshape(count, full)
    z = jnp.zeros((count, full), f32)
    dhn = jnp.zeros((count, full), f32)
    grads1, grads2, bias = [], [], []
    inner = shard.shape[2]
    for j in range(tp):
        q = jnp.dot(hn, gathered[0, j], preferred_element_type=f32) + ch_b1[j * inner : (j + 1) * inner]
        g, g_back = jax.vjp(jax.nn.gelu, q)
        g = g.astype(bf16)
        z = z + jnp.einsum("rh,ch->rc", g, gathered[1, j], preferred_element_type=f32)
        dg = jnp.dot(dz, gathered[1, j], preferred_element_type=f32)
        dq = g_back(dg)[0].astype(bf16)
        grads2.append(jnp.einsum("rc,rh->ch", dz, g, preferred_element_type=f32).astype(bf16))
        grads1.append(jnp.einsum("rc,rh->ch", hn, dq, preferred_element_type=f32).astype(bf16))
        bias.append(jnp.sum(dq.astype(f32), 0))
        dhn = dhn + jnp.einsum("rh,ch->rc", dq, gathered[0, j], preferred_element_type=f32)
    z = (z + ch_b2).astype(bf16).astype(f32).reshape(u.shape)
    block_out = stored((u + z).astype(bf16))
    dhn = dhn.reshape(u.shape)
    dz32 = dz_low.astype(f32)
    image_gain = jnp.sum(dhn * uhat, 1)
    image_shift = jnp.sum(dhn, 1)
    du = dz32 + norm_back(dhn * norms[2], uhat, inv_u)
    dp_low = du.astype(bf16)
    dh = jnp.einsum("nsc,ks->nkc", dp_low, token_w2, preferred_element_type=f32)
    d_tok_w2 = jnp.einsum("nkc,nsc->ks", hidden, dp_low, preferred_element_type=f32)
    d_tok_b2 = jnp.sum(dp_low.astype(f32), (0, 2))
    dpre = hidden_back(dh)[0].astype(bf16)
    d_tok_w1 = jnp.einsum("nsc,nkc->sk", mixed, dpre, preferred_element_type=f32)
    d_tok_b1 = jnp.sum(dpre.astype(f32), (0, 2))
    da = jnp.einsum("nkc,sk->nsc", dpre, token_w1, preferred_element_type=f32)
    d_gain1 = jnp.sum(da * xhat, (0, 1))
    d_shift1 = jnp.sum(da, (0, 1))
    dx = stored((du + norm_back(da * norms[0], xhat, inv_x)).astype(bf16))

    gradient = jnp.stack([jnp.stack(grads1), jnp.stack(grads2)]).reshape(2, tp, dp, rows, inner)
    owned = lax.psum_scatter(lax.psum_scatter(gradient, "tp", scatter_dimension=1, tiled=True).astype(bf16), "dp", scatter_dimension=2, tiled=True)
    owned = owned.astype(f32).reshape(2, rows, inner)

    ids = lax.dynamic_slice_in_dim(group_ids, t * images, images)
    member = (ids[:, None] == jnp.arange(GROUPS)[None, :]).astype(f32)
    groups = jnp.dot(member.T, jnp.concatenate([image_gain, image_shift], 1), precision=highest)
    flat = [d_tok_w1, d_tok_w2, jnp.stack(bias), jnp.sum(dz32, (0, 1)), d_gain1, d_shift1, d_tok_b1, d_tok_b2, groups]
    sizes = [v.size for v in flat]
    need = sum(sizes)
    unit = 64 * full
    padded = -(-need // unit) * unit
    packed = jnp.concatenate([v.reshape(-1) for v in flat] + [jnp.zeros((padded - need,), f32)]).reshape(-1, full)
    total = lax.psum(packed, ("dp", "tp"))
    total = total.reshape(-1)
    pieces, start = [], 0
    for v in flat:
        pieces.append(total[start : start + v.size].reshape(v.shape))
        start += v.size
    tw1, tw2, cb1, cb2, g1, s1, tb1, tb2, gg = pieces
    gg = gg.reshape(GROUPS, 2, full)
    group_norms = jnp.sqrt(jnp.sum(gg * gg, (1, 2)))
    bound = 2.0 * math.sqrt(held * dp * S * full / GROUPS)
    factor = bound / jnp.maximum(group_norms, bound)
    clipped = jnp.sum(factor[:, None, None] * gg, 0)

    def mine(v):
        return lax.dynamic_slice_in_dim(v, t * width, width)

    return (block_out, dx, group_norms, mine(g1), mine(s1), tw1, tb1, tw2, tb2, mine(clipped[0]), mine(clipped[1]),
            owned[0], cb1.reshape(-1), owned[1].T, cb2)


def blocked(block_in, ln1_gain, ln1_shift, tok_w1, tok_b1, tok_w2, tok_b2, ln2_gain, ln2_shift,
            ch_w1, ch_b1, ch_w2, ch_b2, group_ids, out_grad):
    held = block_in.shape[0]
    bound = 2.0 * math.sqrt(held * 8 * S * 768 / GROUPS)
    flat = (held, HALF * 384)
    out, dx, grads, total = one_step(
        ch_w1, ch_w2.T, block_in.reshape(flat), out_grad.reshape(flat), ln1_gain, ln1_shift, ln2_gain, ln2_shift,
        tok_w1, tok_w2.T, tok_b1, tok_b2, ch_b1, ch_b2, group_ids)
    out, dx, d1, d2, tok1, tok2, bias1, bias2, inner, outer, sizes, gain1, shift1, gain2, shift2 = finish(bound, out, dx, grads, total)
    shape = block_in.shape
    return (out.reshape(shape), dx.reshape(shape), sizes, gain1, shift1, tok1, bias1, tok2.T, bias2,
            gain2, shift2, d1, inner, d2.T, outer)


def solution(mesh):
    stored, own, copied = P("dp", "tp", None), P("tp"), P()
    in_specs = (stored, own, own, copied, copied, copied, copied, own, own, P("dp", "tp"), copied, P("tp", "dp"), copied, P("dp"), stored)
    out_specs = (stored, stored, copied, own, own, copied, copied, copied, copied, own, own, P("dp", "tp"), copied, P("tp", "dp"), copied)
    step = blocked if (mesh.shape["dp"], mesh.shape["tp"]) == (8, 4) else general
    return jax.shard_map(step, mesh=mesh, in_specs=in_specs, out_specs=out_specs, check_vma=False)
```

time: 179 us -> 174 us (0.972)
  Pallas kernels: 173 us -> 168 us
    pallas_call x2 -> x1, Pallas kernels: 170 us -> 164 us  [one_step(): pl.pallas_call(step_kernel, out_shape=[sds(packed, BF16), sds(packed, BF1...]
where the time goes in v2:
time: 174 us; the launch traced here: 173 us
  Pallas kernels  168 us (97%)
  local copies, waits for them, and re-layouts  4.68 us (3%)
    pallas_call x1, Pallas kernels, one_step(): pl.pallas_call(step_kernel, out_shape=[sds(packed, BF16), sds(packed, BF1...  164 us
    unnamed x8, local copies, waits for them, and re-layouts  4.68 us
    pallas_call x1, Pallas kernels, finish(): pl.pallas_call(functools.partial(finish_kernel, bound), out_shape=[jax.Sh...  3.53 us

profile of v2, /device:TPU:0, one launch (start us, length us, event | category | flops | bytes accessed | tf_op | source)
XLA Modules:
  0.0 173.5 jit_solution(6878508263199959162)
XLA Ops:
  0.7 164.4 %shard_map.262 = (bf16[4,392,384]{2,1,0:T(8,128)(2,1)}, bf16[4,392,384]{2,1,0:T(8,128)(2,1)}, f32[2,96,768]{2,1,0:T(8,128)}, bf16[384,768]{1,0:T(8,128)(2,1)}) custom-call(f32[96,768]{1,0:T(8,128)} %cw1.1, f32[96,768]{1,0:T(8,128)} %bitcast.11, bf16[16,37632]{1,0:T(8,128)(2,1)} %bitcast.8, bf16[16,37632]{1,0:T(8,128)(2,1)} %bitcast.9, f32[192]{0:T(256)} %p0.1, ...), custom_call_target="tpu_custom_call" | custom-call | tf_op jit(solution)/shard_map/pallas_call | solution.py:672
  165.1 0.0 copy-start
  165.1 1.3 copy-done
  166.4 0.0 copy-start.1
  166.4 1.3 copy-done.1
  167.6 0.0 copy-start.2
  167.6 1.1 copy-done.2
  168.7 0.0 copy-start.3
  168.7 1.1 copy-done.3
  169.8 3.5 %shard_map.263 = (bf16[16,37632]{1,0:T(8,128)(2,1)}, bf16[16,37632]{1,0:T(8,128)(2,1)}, f32[96,768]{1,0:T(8,128)}, f32[96,768]{1,0:T(8,128)}, f32[196,384]{1,0:T...) custom-call(bf16[4,392,384]{2,1,0:T(8,128)(2,1)S(1)} %copy-done, ...), custom_call_target="tpu_custom_call" | custom-call | tf_op jit(solution)/shard_map/pallas_call | solution.py:736
Async XLA Ops:
  165.1 1.3 copy-start
  166.4 1.3 copy-start.1
  167.6 1.1 copy-start.2
  168.7 1.1 copy-start.3

commit v3 on v2

--- a/solution.py
+++ b/solution.py
@@ -137,15 +137,14 @@
 
 PIECE = 48
 SMALL = 8 * PIECE
-DIRECT = (0, 1)
 
 
 def step_kernel(cw1, cw2, xin, din, p0, p1, p2, p3, tw1, tw2, b1, b2, cb1, cb2, ids,
                 o_out, dx_out, w_grad, total_out,
                 wf, shard, wv, stored, xs, ds, xr, dr, flat, xb, u, act, hnt, dzt, g, s, h, ts, zs, lr, lall, t3, c2, w1, w2, w1t, w2t,
-                sib, first, second, final, zz, small, low, t_sib, t_chip, t_line,
+                sib, first, second, final, zz, zi, small, low, t_sib, t_chip, t_line,
                 send_sem, recv_sem, line_sem, x_send, x_recv, d_send, d_recv, ln_send, ln_recv, in_sem, own_sem,
-                o_send, o_recv, y_send, y_recv, sib_sem, sib_recv, a_send, a_recv, z_send, z_recv,
+                o_send, o_recv, y_send, y_recv, sib_sem, sib_recv, a_send, a_recv, z_send, z_recv, i_recv,
                 p_send, p_recv, c_send, c_recv, l_send, l_recv, b_send, b_recv, e_send, e_recv):
     dp, t, near, (y, xx, c) = place()
     line = others(t)
@@ -401,47 +400,43 @@
         total = sib[j, k, 0].astype(F32) + second[j, k].astype(F32) + final[j, k].astype(F32)
         if k < 3:
             sib[j, k, 0] = total.astype(BF16)
-            if j in DIRECT:
-                go(remote(sib.at[j, k, 0], zz.at[j, t], z_send.at[j, k], z_recv.at[j, t], (dp, back[k])))
         else:
             w_grad[j] = total
 
+    inner = (t == 1) | (t == 2)
+    beside = back[2]
+    across = jnp.where(t < 2, 2, 1)
+
     def along_in(j, n):
         remote(zz.at[j, n], zz.at[j, n], z_send.at[j, 0], z_recv.at[j, n], (dp, t)).wait_recv()
 
     def stage_four(j, k):
-        p = back[k]
-        piece = sib.at[j, k, 0]
-        up = remote(piece, zz.at[j, p], z_send.at[j, k], z_recv.at[j, p], (dp, jnp.clip(t + 1, 0, 3)))
-        n = jnp.where(t - 1 == p, 4, p)
-        down = remote(piece, zz.at[j, n], z_send.at[j, k], z_recv.at[j, n], (dp, jnp.clip(t - 1, 0, 3)))
-
-        @pl.when(((p > t) & (t > 0)) | ((p < t) & (t < 3)))
+        piece, p = sib.at[j, k, 0], back[k]
+        if k == 2:
+            go(remote(piece, zz.at[j, t], z_send.at[j, k], z_recv.at[j, t], (dp, p)))
+            return
+        copy = remote(piece, zi.at[j, p % 2], z_send.at[j, k], i_recv.at[j, p % 2], (dp, beside))
+        ends = jnp.logical_not(inner)
+        pl.when(ends)(copy.start)
+        maybe.append((ends, copy))
+
+    def stage_five(j, k):
+        piece, p = sib.at[j, k, 0], back[k]
+        copy = remote(piece, zz.at[j, t], z_send.at[j, k], z_recv.at[j, t], (dp, p))
+
+        @pl.when(inner)
         def _():
-            along_in(j, p)
-            piece[...] = piece[...] + zz[j, p]
-
-        pl.when(p > t)(up.start)
-        pl.when(p < t)(down.start)
-        maybe.append((p > t, up))
-        maybe.append((p < t, down))
-
-    def stage_five(j):
-        if j in DIRECT:
-            for p in line:
-                along_in(j, p)
-                w_grad[j] += zz[j, p].astype(F32)
-            return
-
-        @pl.when(t > 0)
-        def _():
-            along_in(j, t)
-            w_grad[j] += zz[j, t].astype(F32)
-
-        @pl.when(t < 3)
-        def _():
-            along_in(j, 4)
-            w_grad[j] += zz[j, 4].astype(F32)
+            there = zi.at[j, p % 2]
+            remote(there, there, z_send.at[j, k], i_recv.at[j, p % 2], (dp, t)).wait_recv()
+            piece[...] = piece[...] + there[...]
+            copy.start()
+
+        maybe.append((inner, copy))
+
+    def stage_six(j):
+        for n in (beside, across):
+            along_in(j, n)
+            w_grad[j] += zz[j, n].astype(F32)
 
     def second_weight(k):
         wv[1, back[k]] = dot(dzt[...], g[back[k]].reshape(4 * ROWS, 768)).astype(BF16).reshape(8, 96, 768)
@@ -613,44 +608,53 @@
     data(3)
     second_weight(3)
     stage_one(1, 2)
-    stage_one(1, 3)
-    stage_two(1, 0)
-    token_backward(0, 2)
-    stage_two(1, 1)
-    stage_two(1, 2)
-    token_backward(2, 4)
+    token_backward(0, 4)
     pack_dx()
     send_dx(0)
     send_dx(1)
     send_dx(2)
+    stage_one(1, 3)
     total_zero()
+    stage_two(1, 0)
+    stage_two(1, 1)
+    stage_two(1, 2)
     stage_two(1, 3)
+    total_one()
+    first_weight(0)
+    first_weight(1)
+    stage_one(0, 0)
     stage_three(1, 0)
-    first_weight(0)
-    total_one()
-    first_weight(1)
-    stage_three(1, 1)
-    stage_one(0, 0)
+    stage_four(1, 0)
     first_weight(2)
     stage_one(0, 1)
+    stage_three(1, 1)
+    stage_four(1, 1)
     first_weight(3)
     stage_one(0, 2)
     stage_three(1, 2)
+    stage_four(1, 2)
     stage_one(0, 3)
     total_two()
     stage_three(1, 3)
     stage_two(0, 0)
     stage_two(0, 1)
-    total_three()
     stage_two(0, 2)
     stage_two(0, 3)
+    stage_five(1, 0)
+    stage_five(1, 1)
+    total_three()
     stage_three(0, 0)
+    stage_four(0, 0)
     stage_three(0, 1)
+    stage_four(0, 1)
     stage_three(0, 2)
+    stage_four(0, 2)
     stage_three(0, 3)
     total_five()
-    stage_five(1)
-    stage_five(0)
+    stage_five(0, 0)
+    stage_five(0, 1)
+    stage_six(1)
+    stage_six(0)
     total_six()
 
     state["own_o"].wait()
@@ -676,10 +680,10 @@
             V(packed, BF16), V(packed, BF16), V((3, 4 * BLOCK, 128), F32), V(act, BF16), V(act, F32), V(act, BF16), V((768, 4 * ROWS), BF16), V((768, 4 * ROWS), BF16),
             V((4,) + act, BF16), V((4,) + act, BF16), V(tok, BF16), V(tok, BF16), V(act, F32), V((4, 8, 768), F32), V((8, 768), F32),
             V((3, S, 128), F32), V((S, 128), F32), V((ROWS, 384), BF16), V((384, ROWS), BF16), V((384, ROWS), BF16), V((ROWS, 384), BF16),
-            V((2, 4, 4) + piece, BF16), V((2, 4) + piece, BF16), V((2, 4) + piece, BF16), V((2, 4) + piece, BF16), V((2, 5) + piece, BF16),
+            V((2, 4, 4) + piece, BF16), V((2, 4) + piece, BF16), V((2, 4) + piece, BF16), V((2, 4) + piece, BF16), V((2, 4) + piece, BF16), V((2, 2) + piece, BF16),
             V((SMALL, 768), F32), V((SMALL, 768), BF16), V((4 * PIECE, 768), BF16), V((3, PIECE, 768), BF16), V((4, PIECE, 768), BF16),
             dma((28,)), dma((8, 4)), dma((5,)), dma((3,)), dma((4,)), dma((3,)), dma((4,)), dma((3,)), dma((4,)), dma((4,)), dma((2,)),
-            dma((3,)), dma((4,)), dma((3,)), dma((4,)), dma((2, 4, 4)), dma((2, 4, 4)), dma((2, 4, 3)), dma((2, 4, 3)), dma((2, 4)), dma((2, 5)),
+            dma((3,)), dma((4,)), dma((3,)), dma((4,)), dma((2, 4, 4)), dma((2, 4, 4)), dma((2, 4, 3)), dma((2, 4, 3)), dma((2, 4)), dma((2, 4)), dma((2, 2)),
             dma, dma, dma((3,)), dma((3,)), dma((3,)), dma((4,)), dma((3,)), dma((4,)), dma((4,)), dma((4,))],
         compiler_params=pltpu.CompilerParams(collective_id=1, has_side_effects=True, vmem_limit_bytes=63 << 20))(*operands)
 
@@ -738,7 +742,7 @@
         in_specs=[pl.BlockSpec(memory_space=pl.ANY)] * 4, out_specs=[vmem] * len(shapes),
         scratch_shapes=[pltpu.VMEM((4, BLOCK, 384), BF16), pltpu.VMEM((4, BLOCK, 384), BF16), pltpu.VMEM((2, 96, 768), F32), pltpu.VMEM((SMALL, 768), BF16),
             pltpu.VMEM((3, 4 * BLOCK, 128), F32), pltpu.VMEM((3, 4 * BLOCK, 128), F32), pltpu.VMEM((3, S, 128), F32), pltpu.VMEM((SMALL, 768), F32), pltpu.SemaphoreType.DMA((4,))],
-        compiler_params=pltpu.CompilerParams(vmem_limit_bytes=32 << 20))(*operands)
+        compiler_params=pltpu.CompilerParams(vmem_limit_bytes=60 << 20))(*operands)
 
 
 epsilon = 1e-06

time: 174 us -> 164 us (0.943)
  Pallas kernels: 168 us -> 163 us
  local copies, waits for them, and re-layouts: 4.68 us -> 0 us
    pallas_call x1, Pallas kernels: 164 us -> 158 us  [one_step(): pl.pallas_call(step_kernel, out_shape=[sds(packed, BF16), sds(packed, BF1...]
    unnamed x8 -> x0, local copies, waits for them, and re-layouts: 4.68 us -> none
where the time goes in v3:
time: 164 us; the launch traced here: 163 us
  Pallas kernels  163 us (99%)
    pallas_call x1, Pallas kernels, one_step(): pl.pallas_call(step_kernel, out_shape=[sds(packed, BF16), sds(packed, BF1...  158 us
    pallas_call x1, Pallas kernels, finish(): pl.pallas_call(functools.partial(finish_kernel, bound), out_shape=[jax.Sh...  4.62 us

profile of v3, /device:TPU:0, one launch (start us, length us, event | category | flops | bytes accessed | tf_op | source)
XLA Modules:
  0.0 163.4 jit_solution(9280769339630374115)
XLA Ops:
  0.7 158.0 %shard_map.262 = (bf16[4,392,384]{2,1,0:T(8,128)(2,1)}, bf16[4,392,384]{2,1,0:T(8,128)(2,1)}, f32[2,96,768]{2,1,0:T(8,128)}, bf16[384,768]{1,0:T(8,128)(2,1)}) custom-call(f32[96,768]{1,0:T(8,128)} %cw1.1, f32[96,768]{1,0:T(8,128)} %bitcast.11, bf16[16,37632]{1,0:T(8,128)(2,1)} %bitcast.8, bf16[16,37632]{1,0:T(8,128)(2,1)} %bitcast.9, f32[192]{0:T(256)} %p0.1, ...), custom_call_target="tpu_custom_call" | custom-call | tf_op jit(solution)/shard_map/pallas_call | solution.py:676
  158.6 4.6 %shard_map.263 = (bf16[16,37632]{1,0:T(8,128)(2,1)}, bf16[16,37632]{1,0:T(8,128)(2,1)}, f32[96,768]{1,0:T(8,128)}, f32[96,768]{1,0:T(8,128)}, f32[196,384]{1,0:T...) custom-call(bf16[4,392,384]{2,1,0:T(8,128)(2,1)} %get-tuple-element., ...), custom_call_target="tpu_custom_call" | custom-call | tf_op jit(solution)/shard_map/pallas_call | solution.py:740

commit v4 on v3

--- a/solution.py
+++ b/solution.py
@@ -136,11 +136,12 @@
 
 
 PIECE = 48
+DIRECT = (0,)
 SMALL = 8 * PIECE
 
 
 def step_kernel(cw1, cw2, xin, din, p0, p1, p2, p3, tw1, tw2, b1, b2, cb1, cb2, ids,
-                o_out, dx_out, w_grad, total_out,
+                o_out, dx_out, o_fin, dx_fin, w_grad, total_out,
                 wf, shard, wv, stored, xs, ds, xr, dr, flat, xb, u, act, hnt, dzt, g, s, h, ts, zs, lr, lall, t3, c2, w1, w2, w1t, w2t,
                 sib, first, second, final, zz, zi, small, low, t_sib, t_chip, t_line,
                 send_sem, recv_sem, line_sem, x_send, x_recv, d_send, d_recv, ln_send, ln_recv, in_sem, own_sem,
@@ -404,6 +405,7 @@
             w_grad[j] = total
 
     inner = (t == 1) | (t == 2)
+    ends = jnp.logical_not(inner)
     beside = back[2]
     across = jnp.where(t < 2, 2, 1)
 
@@ -412,11 +414,10 @@
 
     def stage_four(j, k):
         piece, p = sib.at[j, k, 0], back[k]
-        if k == 2:
+        if k == 2 or j in DIRECT:
             go(remote(piece, zz.at[j, t], z_send.at[j, k], z_recv.at[j, t], (dp, p)))
             return
         copy = remote(piece, zi.at[j, p % 2], z_send.at[j, k], i_recv.at[j, p % 2], (dp, beside))
-        ends = jnp.logical_not(inner)
         pl.when(ends)(copy.start)
         maybe.append((ends, copy))
 
@@ -434,7 +435,7 @@
         maybe.append((inner, copy))
 
     def stage_six(j):
-        for n in (beside, across):
+        for n in line if j in DIRECT else (beside, across):
             along_in(j, n)
             w_grad[j] += zz[j, n].astype(F32)
 
@@ -501,11 +502,30 @@
             split_groups(lambda r, lane, n=n: zs[n, r : r + HALF, lane : lane + 128], flat, n)
         sent("y")
         pack(flat, ds)
-        state["own_x"] = local(ds.at[t], dx_out.at[t], own_sem.at[1])
+        state["own_x"] = local(ds.at[t], dx_out.at[t], own_sem.at[2])
 
     def send_dx(n):
         p = line[n]
         go(remote(ds.at[p], dx_out.at[t], y_send.at[n], y_recv.at[t], (dp, p)))
+
+    def unpack_output():
+        state["own_o"].wait()
+        for p in line:
+            remote(o_out.at[p], o_out.at[p], o_send.at[0], o_recv.at[p], (dp, t)).wait_recv()
+        local(o_out, dr, own_sem.at[0]).wait()
+        spread(dr, flat)
+        to_stored(flat, stored)
+        state["out"] = local(stored, o_fin, own_sem.at[1])
+
+    def unpack_dx():
+        state["own_x"].wait()
+        for p in line:
+            remote(dx_out.at[p], dx_out.at[p], y_send.at[0], y_recv.at[p], (dp, t)).wait_recv()
+        local(dx_out, xr, own_sem.at[0]).wait()
+        spread(xr, flat)
+        state["out"].wait()
+        to_stored(flat, stored)
+        state["out"] = local(stored, dx_fin, own_sem.at[1])
 
     chip = dp // 2
     far = [("X", near["X"] // 2), ("Y", near["Y"] // 2), ("D", near["D"] // 2)]
@@ -540,15 +560,46 @@
         for n in range(3):
             remote(t_chip.at[n], t_chip.at[n], c_send.at[n], c_recv.at[n], (near["S"], t)).wait_recv()
             total = total + t_chip[n].astype(F32)
-        t_line[t] = total.astype(BF16)
-        for n, p in enumerate(line):
-            go(remote(t_line.at[t], t_line.at[t], l_send.at[n], l_recv.at[t], (dp, p)))
+        part(small, c, chip)[...] = total
+        copy = remote(t_line.at[3], t_line.at[0], l_send.at[0], l_recv.at[0], (dp, beside))
+
+        @pl.when(ends)
+        def _():
+            t_line[3] = total.astype(BF16)
+            copy.start()
+
+        maybe.append((ends, copy))
+
+    def line_wait(n):
+        remote(t_line.at[n], t_line.at[n], l_send.at[0], l_recv.at[n], (dp, t)).wait_recv()
+
+    def total_pair():
+        copy = remote(t_line.at[2], t_line.at[1], l_send.at[1], l_recv.at[1], (dp, across))
+
+        @pl.when(inner)
+        def _():
+            line_wait(0)
+            t_line[2] = (part(small, c, chip)[...] + t_line[0].astype(F32)).astype(BF16)
+            copy.start()
+
+        maybe.append((inner, copy))
+
+    def total_line():
+        copy = remote(own, own, l_send.at[2], l_recv.at[2], (dp, beside))
+
+        @pl.when(inner)
+        def _():
+            line_wait(1)
+            own[...] = (t_line[2].astype(F32) + t_line[1].astype(F32)).astype(BF16)
+            copy.start()
+
+        maybe.append((inner, copy))
 
     def total_three():
-        for p in line:
-            remote(t_line.at[p], t_line.at[p], l_send.at[0], l_recv.at[p], (dp, t)).wait_recv()
-        sums = [t_line[p].astype(F32) for p in range(4)]
-        own[...] = (((sums[0] + sums[1]) + sums[2]) + sums[3]).astype(BF16)
+        @pl.when(ends)
+        def _():
+            remote(own, own, l_send.at[2], l_recv.at[2], (dp, t)).wait_recv()
+
         for n, (name, q) in enumerate(far):
             go(remote(own, own, b_send.at[n], b_recv.at[chip], (near[name], t)))
         go(remote(own, own, e_send.at[3], e_recv.at[chip], (near["S"], t)))
@@ -582,10 +633,10 @@
     neighbours(3)
     diagonal(2)
     diagonal(3)
-    join_input()
     send_grad(0)
     send_grad(1)
     send_grad(2)
+    join_input()
     token_forward(0, 4)
     block(0)
     block(1)
@@ -610,19 +661,20 @@
     stage_one(1, 2)
     token_backward(0, 4)
     pack_dx()
+    total_zero()
     send_dx(0)
     send_dx(1)
     send_dx(2)
     stage_one(1, 3)
-    total_zero()
+    total_one()
     stage_two(1, 0)
     stage_two(1, 1)
     stage_two(1, 2)
     stage_two(1, 3)
-    total_one()
     first_weight(0)
     first_weight(1)
     stage_one(0, 0)
+    total_two()
     stage_three(1, 0)
     stage_four(1, 0)
     first_weight(2)
@@ -634,34 +686,31 @@
     stage_three(1, 2)
     stage_four(1, 2)
     stage_one(0, 3)
-    total_two()
     stage_three(1, 3)
     stage_two(0, 0)
     stage_two(0, 1)
+    unpack_output()
     stage_two(0, 2)
     stage_two(0, 3)
+    total_pair()
     stage_five(1, 0)
     stage_five(1, 1)
-    total_three()
     stage_three(0, 0)
     stage_four(0, 0)
+    total_line()
     stage_three(0, 1)
     stage_four(0, 1)
+    total_three()
     stage_three(0, 2)
     stage_four(0, 2)
     stage_three(0, 3)
+    unpack_dx()
     total_five()
-    stage_five(0, 0)
-    stage_five(0, 1)
     stage_six(1)
     stage_six(0)
     total_six()
 
-    state["own_o"].wait()
-    state["own_x"].wait()
-    for p in line:
-        remote(o_out.at[p], o_out.at[p], o_send.at[0], o_recv.at[p], (dp, t)).wait_recv()
-        remote(dx_out.at[p], dx_out.at[p], y_send.at[0], y_recv.at[p], (dp, t)).wait_recv()
+    state["out"].wait()
     sent("")
     for inside, copy in maybe:
         pl.when(inside)(copy.wait_send)
@@ -674,32 +723,32 @@
     V = pltpu.VMEM
     wshape, act, tok, packed, piece = (2, 4, 8, 96, 768), (4, ROWS, 768), (4, 384, 768), (4, BLOCK, 384), (96, 768)
     return pl.pallas_call(step_kernel,
-        out_shape=[sds(packed, BF16), sds(packed, BF16), sds((2,) + piece, F32), sds((SMALL, 768), BF16)],
-        in_specs=[any_] * 4 + [vmem] * 11, out_specs=[any_] * 2 + [vmem] * 2,
+        out_shape=[sds(packed, BF16), sds(packed, BF16), sds((16, HALF * 384), BF16), sds((16, HALF * 384), BF16), sds((2,) + piece, F32), sds((SMALL, 768), BF16)],
+        in_specs=[any_] * 4 + [vmem] * 11, out_specs=[any_] * 4 + [vmem] * 2,
         scratch_shapes=[V((2, 96, 768), F32), V((2, 96, 768), BF16), V(wshape, BF16), V((16, HALF * 384), BF16), V(packed, BF16), V(packed, BF16),
             V(packed, BF16), V(packed, BF16), V((3, 4 * BLOCK, 128), F32), V(act, BF16), V(act, F32), V(act, BF16), V((768, 4 * ROWS), BF16), V((768, 4 * ROWS), BF16),
             V((4,) + act, BF16), V((4,) + act, BF16), V(tok, BF16), V(tok, BF16), V(act, F32), V((4, 8, 768), F32), V((8, 768), F32),
             V((3, S, 128), F32), V((S, 128), F32), V((ROWS, 384), BF16), V((384, ROWS), BF16), V((384, ROWS), BF16), V((ROWS, 384), BF16),
             V((2, 4, 4) + piece, BF16), V((2, 4) + piece, BF16), V((2, 4) + piece, BF16), V((2, 4) + piece, BF16), V((2, 4) + piece, BF16), V((2, 2) + piece, BF16),
             V((SMALL, 768), F32), V((SMALL, 768), BF16), V((4 * PIECE, 768), BF16), V((3, PIECE, 768), BF16), V((4, PIECE, 768), BF16),
-            dma((28,)), dma((8, 4)), dma((5,)), dma((3,)), dma((4,)), dma((3,)), dma((4,)), dma((3,)), dma((4,)), dma((4,)), dma((2,)),
+            dma((28,)), dma((8, 4)), dma((5,)), dma((3,)), dma((4,)), dma((3,)), dma((4,)), dma((3,)), dma((4,)), dma((4,)), dma((3,)),
             dma((3,)), dma((4,)), dma((3,)), dma((4,)), dma((2, 4, 4)), dma((2, 4, 4)), dma((2, 4, 3)), dma((2, 4, 3)), dma((2, 4)), dma((2, 4)), dma((2, 2)),
             dma, dma, dma((3,)), dma((3,)), dma((3,)), dma((4,)), dma((3,)), dma((4,)), dma((4,)), dma((4,))],
         compiler_params=pltpu.CompilerParams(collective_id=1, has_side_effects=True, vmem_limit_bytes=63 << 20))(*operands)
 
 
-def finish_kernel(bound, o_in, dx_in, grads_in, total_in, o_stored, dx_stored, d1, d2, tok1, tok2, bias1, bias2, inner, outer, sizes, gain1, shift1, gain2, shift2, o, dx, grads, low, flat, wide, t3, total, sems):
+def finish_kernel(bound, o_in, dx_in, grads_in, total_in, o_out, dx_out, d1, d2, tok1, tok2, bias1, bias2, inner, outer, sizes, gain1, shift1, gain2, shift2, o, dx, grads, low, t3, total, sems):
     t = lax.axis_index("tp")
-    copies = [pltpu.make_async_copy(src, dst, sems.at[n]) for n, (src, dst) in enumerate(((total_in, low), (o_in, o), (dx_in, dx), (grads_in, grads)))]
+    copies = [pltpu.make_async_copy(src, dst, sems.at[n]) for n, (src, dst) in enumerate(((o_in, o), (dx_in, dx), (total_in, low), (grads_in, grads)))]
     for copy in copies:
         copy.start()
-    for copy in copies:
-        copy.wait()
+    for n, (src, dst) in enumerate(((o, o_out), (dx, dx_out))):
+        copies[n].wait()
+        copies[n] = pltpu.make_async_copy(src, dst, sems.at[4 + n])
+        copies[n].start()
+    copies[2].wait()
+    copies[3].wait()
     total[...] = low[...].astype(F32)
-    spread(o, flat)
-    to_stored(flat, o_stored)
-    spread(dx, wide)
-    to_stored(wide, dx_stored)
     d1[...] = grads[0]
     d2[...] = grads[1]
     for start, dst in ((0, tok1), (384, tok2)):
@@ -732,6 +781,8 @@
     own(total[203:204, :], shift1)
     own(jnp.sum(factor * gg, 0, keepdims=True), gain2)
     own(jnp.sum(factor * gb, 0, keepdims=True), shift2)
+    copies[0].wait()
+    copies[1].wait()
 
 
 def finish(bound, *operands):
@@ -739,9 +790,8 @@
     shapes = [(16, HALF * 384)] * 2 + [(96, 768)] * 2 + [(S, 384)] * 2 + [(384,), (S,), (3072,), (768,), (GROUPS,)] + [(192,)] * 4
     return pl.pallas_call(functools.partial(finish_kernel, bound),
         out_shape=[jax.ShapeDtypeStruct(v, BF16 if n < 2 else F32) for n, v in enumerate(shapes)],
-        in_specs=[pl.BlockSpec(memory_space=pl.ANY)] * 4, out_specs=[vmem] * len(shapes),
-        scratch_shapes=[pltpu.VMEM((4, BLOCK, 384), BF16), pltpu.VMEM((4, BLOCK, 384), BF16), pltpu.VMEM((2, 96, 768), F32), pltpu.VMEM((SMALL, 768), BF16),
-            pltpu.VMEM((3, 4 * BLOCK, 128), F32), pltpu.VMEM((3, 4 * BLOCK, 128), F32), pltpu.VMEM((3, S, 128), F32), pltpu.VMEM((SMALL, 768), F32), pltpu.SemaphoreType.DMA((4,))],
+        in_specs=[pl.BlockSpec(memory_space=pl.ANY)] * 4, out_specs=[pl.BlockSpec(memory_space=pl.ANY)] * 2 + [vmem] * (len(shapes) - 2),
+        scratch_shapes=[pltpu.VMEM((16, HALF * 384), BF16), pltpu.VMEM((16, HALF * 384), BF16), pltpu.VMEM((2, 96, 768), F32), pltpu.VMEM((SMALL, 768), BF16), pltpu.VMEM((3, S, 128), F32), pltpu.VMEM((SMALL, 768), F32), pltpu.SemaphoreType.DMA((6,))],
         compiler_params=pltpu.CompilerParams(vmem_limit_bytes=60 << 20))(*operands)
 
 
@@ -872,7 +922,7 @@
     held = block_in.shape[0]
     bound = 2.0 * math.sqrt(held * 8 * S * 768 / GROUPS)
     flat = (held, HALF * 384)
-    out, dx, grads, total = one_step(
+    _, _, out, dx, grads, total = one_step(
         ch_w1, ch_w2.T, block_in.reshape(flat), out_grad.reshape(flat), ln1_gain, ln1_shift, ln2_gain, ln2_shift,
         tok_w1, tok_w2.T, tok_b1, tok_b2, ch_b1, ch_b2, group_ids)
     out, dx, d1, d2, tok1, tok2, bias1, bias2, inner, outer, sizes, gain1, shift1, gain2, shift2 = finish(bound, out, dx, grads, total)

time: 164 us -> 160 us (0.976); the launches traced: 163 us -> 158 us
  Pallas kernels: 163 us -> 157 us
    pallas_call x1, Pallas kernels: 158 us -> 153 us  [one_step(): pl.pallas_call(step_kernel, out_shape=[sds(packed, BF16), sds(packed, BF1...]
where the time goes in v4:
time: 160 us; the launch traced here: 158 us
  Pallas kernels  157 us (98%)
    pallas_call x1, Pallas kernels, one_step(): pl.pallas_call(step_kernel, out_shape=[sds(packed, BF16), sds(packed, BF1...  153 us
    pallas_call x1, Pallas kernels, finish(): pl.pallas_call(functools.partial(finish_kernel, bound), out_shape=[jax.Sh...  3.8 us

profile of v4, /device:TPU:0, one launch (start us, length us, event | category | flops | bytes accessed | tf_op | source)
XLA Modules:
  0.0 157.7 jit_solution(13474030173665092401)
XLA Ops:
  0.7 153.1 %shard_map.262 = (bf16[4,392,384]{2,1,0:T(8,128)(2,1)}, bf16[4,392,384]{2,1,0:T(8,128)(2,1)}, bf16[16,37632]{1,0:T(8,128)(2,1)}, bf16[16,37632]{1,0:T(8,128)(2,1...) custom-call(f32[96,768]{1,0:T(8,128)} %cw1.1, f32[96,768]{1,0:T(8,128)} %bitcast.11, bf16[16,37632]{1,0:T(8,128)(2,1)} %bitcast.8, ...), custom_call_target="tpu_custom_call" | custom-call | tf_op jit(solution)/shard_map/pallas_call | solution.py:725
  153.8 3.8 %shard_map.263 = (bf16[16,37632]{1,0:T(8,128)(2,1)}, bf16[16,37632]{1,0:T(8,128)(2,1)}, f32[96,768]{1,0:T(8,128)}, f32[96,768]{1,0:T(8,128)}, f32[196,384]{1,0:T...) custom-call(bf16[16,37632]{1,0:T(8,128)(2,1)} %get-tuple-element.34., ...), custom_call_target="tpu_custom_call" | custom-call | tf_op jit(solution)/shard_map/pallas_call | solution.py:791
